TPU v7x, 512 devices: a whole 4x4x16 slice. The times are simulated.
512 devices in a mesh: seq: 128 (over z, x, core), head: 4 (over y).
Axes of the slice: x: 4, y: 4, z: 16, core: 2. Of those that a mesh axis runs over, the one named last changes fastest.
Arguments:
- loader_rows: bfloat16 [65536, 1536], P('seq', 'head'), may hold values from -36 to 36
- plan: int32 [128, 128], replicated, may hold values from 0 to 4, as said below
- lengths: int32 [170], replicated, may hold values from 1 to 1024, 32768 in all
- gain: float32 [1536], replicated, may hold values from 0.1 to 1.9
- wq: bfloat16 [1536, 1536], P(None, 'head'), may hold values from -1.6 to 1.6
- wk: bfloat16 [1536, 1536], P(None, 'head'), may hold values from -1.6 to 1.6
- wv: bfloat16 [1536, 1536], P(None, 'head'), may hold values from -0.15625 to 0.15625
- conv_weight: float32 [31, 1536], P(None, 'head'), may hold values from -1 to 1
- cotangent: bfloat16 [32768, 1536], P('seq', 'head'), may hold values from -6 to 6
Outputs:
- output: bfloat16 [32768, 1536], P('seq', 'head')
- grad_input: bfloat16 [32768, 1536], P('seq', 'head')
Inputs may be any that keep to these rules, and one draw needn't show every extreme that they name: plan[s, d] rows go from loader shard s to frame shard d, taken from the start of block (s, d); every row and every column of the plan sums to 256 and holds the same counts as every other row and column, in another order; some entries equal 4. `lengths`: the utterances cover the 32768 frames in order; the longest has exactly 1024 frames.
All inputs are finite; a program needn't handle non-finite values.
Results may differ from a plain program's by a relative error of at most 0.024.
The roundings to bfloat16 on the way count: a program that leaves them out, or rounds other values in their place, can miss the bound.
Values may be sent and summed in bfloat16 or wider, within the bound.
A program may use at most 64 MiB of HBM per device.

v0:
```python
import math

import jax
import jax.numpy as jnp
from jax import lax
from jax.sharding import PartitionSpec as P

HEAD_DIM = 64
KS = 31
HALF_K = 15
WIN = 256


EPSILON = 1e-05


def extended_2(shard, sides, width):
    for axis, dim in sides:
        size, length = (lax.axis_size(axis), shard.shape[dim])
        up = [(i, (i + 1) % size) for i in range(size - 1)]
        down = [(j, i) for i, j in up]
        last = lax.slice_in_dim(shard, length - width, length, axis=dim)
        leading = lax.slice_in_dim(shard, 0, width, axis=dim)
        before = lax.ppermute(last, axis, up)
        after = lax.ppermute(leading, axis, down)
        shard = jnp.concatenate([before, shard, after], axis=dim)
    return shard


def from_behind(shard, axis, by):
    size = lax.axis_size(axis)
    pairs = [(i, i + by) for i in range(size) if 0 <= i + by < size]
    return lax.ppermute(shard, axis, pairs)


def segment_ids(positions, lengths, frame_total):
    utter_ends = jnp.cumsum(lengths)
    inside = (positions >= 0) & (positions < frame_total)
    counted = jnp.sum((utter_ends[None, :] <= positions[:, None]).astype(jnp.int32), axis=1)
    return jnp.where(inside, counted, -1)


def back_project(grad_part, weight):
    return lax.dot_general(
        grad_part, weight, (((1,), (1,)), ((), ())), preferred_element_type=jnp.float32
    )


def on_device(loader_rows, plan, lengths, gain, wq, wk, wv, conv_weight, cotangent):
    seq_count = lax.axis_size("seq")
    seq_index = lax.axis_index("seq")
    frames, part_cols = cotangent.shape
    head_count = part_cols // HEAD_DIM
    frame_total = frames * seq_count
    capacity = loader_rows.shape[0] // seq_count
    column_start = lax.axis_index("head") * part_cols
    score_scale = 1.0 / math.sqrt(HEAD_DIM)
    blocks = loader_rows.reshape(seq_count, capacity, part_cols)
    arrived = lax.all_to_all(blocks, "seq", split_axis=0, concat_axis=0, tiled=True)
    counts = lax.dynamic_slice_in_dim(plan, seq_index, 1, 1)[:, 0]
    running = jnp.cumsum(counts)
    slot_index = jnp.arange(frames, dtype=jnp.int32)
    source = jnp.sum((running[None, :] <= slot_index[:, None]).astype(jnp.int32), axis=1)
    earlier = jnp.arange(seq_count, dtype=jnp.int32)[None, :] < source[:, None]
    before = jnp.sum(jnp.where(earlier, counts[None, :], 0), axis=1)
    row_index = source * capacity + slot_index - before
    frame_part = jnp.take(arrived.reshape(seq_count * capacity, part_cols), row_index, axis=0)
    gathered = lax.all_gather(frame_part, "head", axis=1, tiled=True)
    values = gathered.astype(jnp.float32)
    row_mean = jnp.mean(values, axis=1, keepdims=True)
    centred = values - row_mean
    inverse_std = lax.rsqrt(jnp.mean(centred * centred, axis=1, keepdims=True) + EPSILON)
    unit_rows = centred * inverse_std
    normed = (unit_rows * gain[None, :]).astype(jnp.bfloat16)
    queries = jnp.dot(normed, wq, preferred_element_type=jnp.float32).astype(jnp.bfloat16)
    key_rows = jnp.dot(normed, wk, preferred_element_type=jnp.float32).astype(jnp.bfloat16)
    value_rows = jnp.dot(normed, wv, preferred_element_type=jnp.float32).astype(jnp.bfloat16)
    stacked = jnp.stack([key_rows, value_rows], axis=1)
    extended = extended_2(stacked, (("seq", 0),), WIN)
    span = frames + 2 * WIN
    key_heads = extended[:, 0].reshape(span, head_count, HEAD_DIM)
    value_heads = extended[:, 1].reshape(span, head_count, HEAD_DIM)
    query_heads = queries.reshape(frames, head_count, HEAD_DIM)
    positions = seq_index * frames + jnp.arange(-WIN, frames + WIN, dtype=jnp.int32)
    segments = segment_ids(positions, lengths, frame_total)
    query_seg = segments[WIN : WIN + frames]
    offset = jnp.arange(span, dtype=jnp.int32)[None, :] - (
        jnp.arange(frames, dtype=jnp.int32)[:, None] + WIN
    )
    allowed = (offset >= -WIN) & (offset < WIN) & (segments[None, :] == query_seg[:, None])
    scores = (
        jnp.einsum("qhe,khe->hqk", query_heads, key_heads, preferred_element_type=jnp.float32)
        * score_scale
    )
    masked = jnp.where(allowed[None, :, :], scores, -jnp.inf)
    row_max = jnp.max(masked, axis=2, keepdims=True)
    lifted = jnp.exp(masked - row_max)
    row_total = jnp.sum(lifted, axis=2, keepdims=True)
    weights = lifted / row_total
    weights_low = weights.astype(jnp.bfloat16)
    attended = jnp.einsum(
        "hqk,khe->qhe", weights_low, value_heads, preferred_element_type=jnp.float32
    )
    residual = (frame_part.astype(jnp.float32) + attended.reshape(frames, part_cols)).astype(
        jnp.bfloat16
    )
    conv_seg = segments[WIN - HALF_K : WIN + frames + HALF_K]
    residual_pad = extended_2(residual, (("seq", 0),), HALF_K)
    conv_out = jnp.zeros((frames, part_cols), jnp.float32)
    for kernel_tap in range(KS):
        same_seg = (conv_seg[kernel_tap : kernel_tap + frames] == query_seg)[:, None]
        conv_out = conv_out + jnp.where(
            same_seg,
            residual_pad[kernel_tap : kernel_tap + frames].astype(jnp.float32)
            * conv_weight[kernel_tap][None, :],
            0.0,
        )
    sigmoid_gate = jax.nn.sigmoid(conv_out)
    output = (residual.astype(jnp.float32) + conv_out * sigmoid_gate).astype(jnp.bfloat16)
    upstream_all = cotangent.astype(jnp.float32)
    grad_conv = (upstream_all * sigmoid_gate * (1.0 + conv_out * (1.0 - sigmoid_gate))).astype(
        jnp.bfloat16
    )
    grad_pad = extended_2(grad_conv, (("seq", 0),), HALF_K)
    transposed = jnp.zeros((frames, part_cols), jnp.float32)
    for kernel_tap in range(KS):
        mirror = KS - 1 - kernel_tap
        same_seg = (conv_seg[mirror : mirror + frames] == query_seg)[:, None]
        transposed = transposed + jnp.where(
            same_seg,
            grad_pad[mirror : mirror + frames].astype(jnp.float32)
            * conv_weight[kernel_tap][None, :],
            0.0,
        )
    grad_residual = (upstream_all + transposed).astype(jnp.bfloat16)
    upstream = grad_residual.reshape(frames, head_count, HEAD_DIM)
    row_delta = jnp.sum(upstream.astype(jnp.float32) * attended, axis=2)
    grad_weights = jnp.einsum(
        "qhe,khe->hqk", upstream, value_heads, preferred_element_type=jnp.float32
    )
    grad_scores = (
        weights * (grad_weights - jnp.transpose(row_delta)[:, :, None]) * score_scale
    ).astype(jnp.bfloat16)
    grad_query = (
        jnp.einsum("hqk,khe->qhe", grad_scores, key_heads, preferred_element_type=jnp.float32)
        .reshape(frames, part_cols)
        .astype(jnp.bfloat16)
    )
    grad_keys = jnp.einsum(
        "hqk,qhe->khe", grad_scores, query_heads, preferred_element_type=jnp.float32
    ).reshape(span, part_cols)
    grad_values = jnp.einsum(
        "hqk,qhe->khe", weights_low, upstream, preferred_element_type=jnp.float32
    ).reshape(span, part_cols)
    kv_grads = jnp.stack([grad_keys, grad_values], axis=1)
    from_right = from_behind(kv_grads[:WIN], "seq", -1)
    from_left = from_behind(kv_grads[frames + WIN :], "seq", 1)
    own_grads = kv_grads[WIN : WIN + frames]
    own_grads = own_grads + from_left
    own_grads = own_grads + from_right
    grad_key_low = own_grads[:, 0].astype(jnp.bfloat16)
    grad_value_low = own_grads[:, 1].astype(jnp.bfloat16)
    grad_normed = (
        back_project(grad_query, wq)
        + back_project(grad_key_low, wk)
        + back_project(grad_value_low, wv)
    )
    grad_whole = lax.psum(grad_normed, "head")
    scaled = grad_whole * gain[None, :]
    mean_term = jnp.mean(scaled, axis=1, keepdims=True)
    slope_term = jnp.mean(scaled * unit_rows, axis=1, keepdims=True)
    through_all = inverse_std * (scaled - mean_term - unit_rows * slope_term)
    through = lax.dynamic_slice_in_dim(through_all, column_start, part_cols, 1)
    grad_input = (grad_residual.astype(jnp.float32) + through).astype(jnp.bfloat16)
    return (output, grad_input)


def solution(mesh):
    placed = (
        P("seq", "head"),
        P(),
        P(),
        P(),
        P(None, "head"),
        P(None, "head"),
        P(None, "head"),
        P(None, "head"),
        P("seq", "head"),
    )
    return jax.shard_map(
        on_device,
        mesh=mesh,
        in_specs=placed,
        out_specs=(P("seq", "head"), P("seq", "head")),
        check_vma=False,
    )
```

profile of v0, /device:TPU:1, one launch (start us, length us, event | category | flops | bytes accessed | tf_op | source)
XLA Modules:
  0.0 239.7 jit_solution(10754253917114190334)
XLA Ops:
  7.2 1.9 reshape.225
  9.1 20.4 %all-to-all-start = ((bf16[128,4,384]{2,1,0:T(4,128)(2,1)}), bf16[128,4,384]{2,1,0:T(4,128)(2,1)S(1)}, u32[]{:S(2)}, u32[]{:S(2)}) async-start(bf16[128,4,384]{2,1,0:T(4,128)(2,1)} %reshape.225), calls=%async_computation | async-start | bytes 786432 | tf_op jit(solution)/shard_map/all_to_all | solution.py:59
  34.4 20.6 %all-to-all-done = bf16[128,4,384]{2,1,0:T(4,128)(2,1)S(1)} async-done(((bf16[128,4,384]{2,1,0:T(4,128)(2,1)}), bf16[128,4,384]{2,1,0:T(4,128)(2,1)S(1)}, u32[]{:S(2)}, u32[]{:S(2)}) %all-to-all-start) | async-done | bytes 393248 | tf_op jit(solution)/shard_map/all_to_all | solution.py:59
  55.1 1.2 gather_fusion
  56.4 13.3 %all_gather.3 = bf16[256,1536]{1,0:T(8,128)(2,1)S(1)} all-gather(bf16[256,384]{1,0:T(8,128)(2,1)S(1)} %broadcast_select_fusion), channel_id=1, replica_groups=mesh['seq'=128,'head'=4] {'head'}, dimensions={1}, use_global_device_ids=true | all-gather | bytes 983040 | tf_op jit(solution)/shard_map/all_gather | solution.py:68
  72.3 4.2 %collective-permute-start.1 = (bf16[256,2,384]{2,0,1:T(8,128)(2,1)S(1)}, bf16[256,2,384]{2,0,1:T(8,128)(2,1)S(1)}, u32[]{:S(2)}, u32[]{:S(2)}) collective-permute-start(bf16[256,2,384]{2,0,1:T(8,128)(2,1)S(1)} %pad_maximum_fusion.2), channel_id=1, source_target_pairs={{4,0},{8,4},{12,8},{16,12},{20,16},{24,20},{28,24},{32,28},{36,32}... | collective-permute-start | bytes 1179656 | tf_op jit(solution)/shard_map/ppermute | solution.py:25
  76.5 4.5 %collective-permute-start = (bf16[256,2,384]{2,0,1:T(8,128)(2,1)S(1)}, bf16[256,2,384]{2,0,1:T(8,128)(2,1)S(1)}, u32[]{:S(2)}, u32[]{:S(2)}) collective-permute-start(bf16[256,2,384]{2,0,1:T(8,128)(2,1)S(1)} %pad_maximum_fusion.2), channel_id=1, source_target_pairs={{0,4},{4,8},{8,12},{12,16},{16,20},{20,24},{24,28},{28,32},{32,36}... | collective-permute-start | bytes 1179656 | tf_op jit(solution)/shard_map/ppermute | solution.py:24
  82.5 2.0 collective-permute-done.1
  84.5 1.2 collective-permute-done
  86.2 1.1 copy.24
  87.3 4.4 %fusion.111 = (f32[6,256]{1,0:T(8,128)}, f32[6,256,768]{2,1,0:T(8,128)}) fusion(pred[256,768]{1,0:T(8,128)(4,1)S(1)} %fusion.19, bf16[256,6,64]{0,2,1:T(8,128)(2,1)S(1)} %bitcast.71, bf16[768,6,64]{0,2,1:T(8,128)(2,1)S(1)} %bitcast.66), kind=kOutput, calls=%fused_computation.321 | convolution fusion | flops 155714304 | bytes 5707776 | tf_op jit(solution)/shard_map/sub | solution.py:97
  91.7 2.8 %fusion.5 = bf16[6,256,768]{2,1,0:T(8,128)(2,1)S(1)} fusion(f32[6,256,768]{2,1,0:T(8,128)} %get-tuple-element.80, f32[6,256]{1,0:T(8,128)} %get-tuple-element.79), kind=kLoop, calls=%fused_computation.18 | loop fusion | flops 2359296 | bytes 7084032 | tf_op jit(solution)/shard_map/convert_element_type | solution.py:100
  94.5 1.6 fusion.112
  96.1 1.9 copy.27
  98.0 1.2 add_convert_fusion
  99.3 4.4 %collective-permute-start.2 = (bf16[15,384]{1,0:T(8,128)(2,1)S(1)}, bf16[15,384]{1,0:T(8,128)(2,1)S(1)}, u32[]{:S(2)}, u32[]{:S(2)}) collective-permute-start(bf16[15,384]{1,0:T(8,128)(2,1)S(1)} %get-tuple-element.47), channel_id=1, source_target_pairs={{0,4},{4,8},{8,12},{12,16},{16,20},{20,24},{24,28},{28,32},{32,36}... | collective-permute-start | bytes 34568 | tf_op jit(solution)/shard_map/ppermute | solution.py:24
  103.7 2.1 collective-permute-start.3
  106.9 1.9 collective-permute-done.3
  108.7 5.4 %fusion.40 = (bf16[256,384]{1,0:T(8,128)(2,1)S(1)}, f32[256,384]{1,0:T(8,128)}) fusion(bf16[256,384]{1,0:T(8,128)(2,1)} %param.17, f32[384]{0:T(512)S(1)} %get-tuple-element.33, bf16[15,384]{1,0:T(8,128)(2,1)S(1)} %collective-permute-done.3, bf16[256,384]{1,0:T(8,128)(2,1)S(1)} %add_convert_fusion, pred[256]{0:T(512)(128)(4,1)} %get-tuple-element.50, ...), kind=kLoop, calls=%fused_computation.123 | loop fusion | flops 21823488 | bytes 1061376 | tf_op jit(solution)/shard_map/convert_element_type | solution.py:121
  114.1 1.9 collective-permute-start.4
  116.1 3.6 %collective-permute-start.5 = (bf16[15,384]{1,0:T(8,128)(2,1)S(1)}, bf16[15,384]{1,0:T(8,128)(2,1)S(1)}, u32[]{:S(2)}, u32[]{:S(2)}) collective-permute-start(bf16[15,384]{1,0:T(8,128)(2,1)S(1)} %get-tuple-element.46), channel_id=1, source_target_pairs={{0,4},{4,8},{8,12},{12,16},{16,20},{20,24},{24,28},{28,32},{32,36}... | collective-permute-start | bytes 34568 | tf_op jit(solution)/shard_map/ppermute | solution.py:24
  120.5 5.2 %fusion.41 = bf16[256,384]{1,0:T(8,128)(2,1)} fusion(bf16[256,384]{1,0:T(8,128)(2,1)S(1)} %copy-done.20, bf16[256,384]{1,0:T(8,128)(2,1)S(1)} %get-tuple-element.36, bf16[15,384]{1,0:T(8,128)(2,1)S(1)} %collective-permute-done.5, bf16[15,384]{1,0:T(8,128)(2,1)S(1)} %collective-permute-done.4, f32[384]{0:T(512)S(1)} %get-tuple-element.33, ...), kind=kLoop, calls=%fused_computation.124 | loop fusion | flops 21135360 | bytes 668160 | tf_op jit(solution)/shard_map/convert_element_type | solution.py:135
  125.8 1.7 copy.28
  127.5 1.6 fusion.115
  129.2 3.0 %multiply_convert_fusion = bf16[6,256,768]{2,1,0:T(8,128)(2,1)S(1)} fusion(f32[6,256]{1,0:T(8,128)S(1)} %bitcast.75, bf16[256,6,64]{0,2,1:T(8,128)(2,1)S(1)} %bitcast.70, bf16[768,6,64]{0,2,1:T(8,128)(2,1)S(1)} %bitcast.65, f32[6,256,768]{2,1,0:T(8,128)} %get-tuple-element.80, f32[6,256]{1,0:T(8,128)S(1)} %copy-done.29), kind=kOutput, calls=%fused_computation.2 | convolution fusion | flops 156893184 | bytes 7876608 | tf_op jit(solution)/shard_map/qhe,khe->hqk/dot_general | solution.py:138
  132.9 4.3 %collective-permute-start.6 = (f32[256,2,384]{0,2,1:T(8,128)S(1)}, f32[256,2,384]{0,2,1:T(8,128)S(1)}, u32[]{:S(2)}, u32[]{:S(2)}) collective-permute-start(f32[256,2,384]{0,2,1:T(8,128)S(1)} %get-tuple-element.40), channel_id=1, source_target_pairs={{0,4},{4,8},{8,12},{12,16},{16,20},{20,24},{24,28},{28,32},{32,36}... | collective-permute-start | bytes 2359304 | tf_op jit(solution)/shard_map/ppermute | solution.py:33
  137.3 1.9 collective-permute-start.7
  140.7 5.5 %collective-permute-done.6 = f32[256,2,384]{0,2,1:T(8,128)S(1)} collective-permute-done((f32[256,2,384]{0,2,1:T(8,128)S(1)}, f32[256,2,384]{0,2,1:T(8,128)S(1)}, u32[]{:S(2)}, u32[]{:S(2)}) %collective-permute-start.6) | collective-permute-done | bytes 786464 | tf_op jit(solution)/shard_map/ppermute | solution.py:33
  146.2 4.4 %collective-permute-done.7 = f32[256,2,384]{0,2,1:T(8,128)S(1)} collective-permute-done((f32[256,2,384]{0,2,1:T(8,128)S(1)}, f32[256,2,384]{0,2,1:T(8,128)S(1)}, u32[]{:S(2)}, u32[]{:S(2)}) %collective-permute-start.7) | collective-permute-done | bytes 786464 | tf_op jit(solution)/shard_map/ppermute | solution.py:33
  152.1 1.8 convolution_add_fusion
  155.7 74.3 %all-reduce.3.cloned.1.call-done = f32[256,1536]{1,0:T(8,128)} async-done(((f32[256,1536]{1,0:T(8,128)}), f32[256,1536]{1,0:T(8,128)}) %all-reduce.3.cloned.1.call-update) | async-done | bytes 1572880 | tf_op jit(solution)/shard_map/psum | solution.py:168
  230.1 1.9 fusion.105
  (122 shorter events, 17.8 us)
Async XLA Ops:
  7.2 74.5 %copy-start = (bf16[1536,384]{1,0:T(8,128)(2,1)S(1)}, bf16[1536,384]{1,0:T(8,128)(2,1)}, u32[]{:S(2)}) copy-start(bf16[1536,384]{1,0:T(8,128)(2,1)} %param.13) | copy-start | bytes 3538948
  7.2 22.4 %copy-start.31 = (s32[170]{0:T(256)S(1)}, s32[170]{0:T(256)}, u32[]{:S(2)}) copy-start(s32[170]{0:T(256)} %param.11) | copy-start | bytes 2044
  7.2 23.2 %copy-start.21 = (s32[128,128]{1,0:T(8,128)S(1)}, s32[128,128]{1,0:T(8,128)}, u32[]{:S(2)}) copy-start(s32[128,128]{1,0:T(8,128)} %param.10) | copy-start | bytes 196612
  9.1 45.9 %all-to-all-start = ((bf16[128,4,384]{2,1,0:T(4,128)(2,1)}), bf16[128,4,384]{2,1,0:T(4,128)(2,1)S(1)}, u32[]{:S(2)}, u32[]{:S(2)}) async-start(bf16[128,4,384]{2,1,0:T(4,128)(2,1)} %reshape.225), calls=%async_computation | async-start | bytes 786432 | tf_op jit(solution)/shard_map/all_to_all | solution.py:59
  29.5 200.5 %all-reduce.3.cloned.1.call-start = ((), (), s32[]{:S(2)}) async-start(), calls=%async_computation.1 | async-start | bytes 3145728 | tf_op jit(solution)/shard_map/psum | solution.py:168
  31.2 25.2 %copy-start.30 = (pred[256]{0:T(512)(128)(4,1)}, pred[256]{0:T(512)(128)(4,1)S(1)}, u32[]{:S(2)}) copy-start(pred[256]{0:T(512)(128)(4,1)S(1)} %compare_and_fusion) | copy-start | bytes 772
  56.2 14.7 %copy-start.12 = (bf16[256,384]{1,0:T(8,128)(2,1)}, bf16[256,384]{1,0:T(8,128)(2,1)S(1)}, u32[]{:S(2)}) copy-start(bf16[256,384]{1,0:T(8,128)(2,1)S(1)} %gather_fusion) | copy-start | bytes 589828
  56.2 14.0 %copy-start.14 = (bf16[1536,384]{1,0:T(8,128)(2,1)S(1)}, bf16[1536,384]{1,0:T(8,128)(2,1)}, u32[]{:S(2)}) copy-start(bf16[1536,384]{1,0:T(8,128)(2,1)} %param.14) | copy-start | bytes 3538948
  56.3 14.0 %copy-start.27 = (f32[1536]{0:T(1024)S(1)}, f32[1536]{0:T(1024)}, u32[]{:S(2)}) copy-start(f32[1536]{0:T(1024)} %param.12) | copy-start | bytes 18436
  69.7 12.0 %copy-start.1 = (bf16[256,1536]{1,0:T(8,128)(2,1)}, bf16[256,1536]{1,0:T(8,128)(2,1)S(1)}, u32[]{:S(2)}) copy-start(bf16[256,1536]{1,0:T(8,128)(2,1)S(1)} %all_gather.3) | copy-start | bytes 2359300
  69.9 11.8 %copy-start.25 = (f32[256]{0:T(256)}, f32[256]{0:T(256)S(1)}, u32[]{:S(2)}) copy-start(f32[256]{0:T(256)S(1)} %broadcast_multiply_fusion.3) | copy-start | bytes 3076
  70.3 11.4 %copy-start.23 = (f32[256]{0:T(256)}, f32[256]{0:T(256)S(1)}, u32[]{:S(2)}) copy-start(f32[256]{0:T(256)S(1)} %add_rsqrt_fusion) | copy-start | bytes 3076
  71.6 9.4 %copy-start.22 = (f32[31,384]{1,0:T(8,128)S(1)}, f32[31,384]{1,0:T(8,128)}, u32[]{:S(2)}) copy-start(f32[31,384]{1,0:T(8,128)} %param.16) | copy-start | bytes 142852
  72.3 12.2 %collective-permute-start.1 = (bf16[256,2,384]{2,0,1:T(8,128)(2,1)S(1)}, bf16[256,2,384]{2,0,1:T(8,128)(2,1)S(1)}, u32[]{:S(2)}, u32[]{:S(2)}) collective-permute-start(bf16[256,2,384]{2,0,1:T(8,128)(2,1)S(1)} %pad_maximum_fusion.2), channel_id=1, source_target_pairs={{4,0},{8,4},{12,8},{16,12},{20,16},{24,20},{28,24},{32,28},{36,32}... | collective-permute-start | bytes 1179656 | tf_op jit(solution)/shard_map/ppermute | solution.py:25
  76.5 9.2 %collective-permute-start = (bf16[256,2,384]{2,0,1:T(8,128)(2,1)S(1)}, bf16[256,2,384]{2,0,1:T(8,128)(2,1)S(1)}, u32[]{:S(2)}, u32[]{:S(2)}) collective-permute-start(bf16[256,2,384]{2,0,1:T(8,128)(2,1)S(1)} %pad_maximum_fusion.2), channel_id=1, source_target_pairs={{0,4},{4,8},{8,12},{12,16},{16,20},{20,24},{24,28},{28,32},{32,36}... | collective-permute-start | bytes 1179656 | tf_op jit(solution)/shard_map/ppermute | solution.py:24
  82.5 4.8 %copy-start.18 = (bf16[256,384]{0,1:T(8,128)(2,1)}, bf16[256,384]{0,1:T(8,128)(2,1)S(1)}, u32[]{:S(2)}) copy-start(bf16[256,384]{0,1:T(8,128)(2,1)S(1)} %copy.25) | copy-start | bytes 589828
  86.2 5.6 %copy-start.6 = (bf16[768,1,384]{0,2,1:T(8,128)(2,1)}, bf16[768,1,384]{0,2,1:T(8,128)(2,1)S(1)}, u32[]{:S(2)}) copy-start(bf16[768,1,384]{0,2,1:T(8,128)(2,1)S(1)} %copy.26) | copy-start | bytes 1769476
  98.0 22.5 %copy-start.20 = (bf16[256,384]{1,0:T(8,128)(2,1)S(1)}, bf16[256,384]{1,0:T(8,128)(2,1)}, u32[]{:S(2)}) copy-start(bf16[256,384]{1,0:T(8,128)(2,1)} %param.17) | copy-start | bytes 589828
  99.3 9.4 %copy-start.8 = (bf16[256,384]{1,0:T(8,128)(2,1)}, bf16[256,384]{1,0:T(8,128)(2,1)S(1)}, u32[]{:S(2)}) copy-start(bf16[256,384]{1,0:T(8,128)(2,1)S(1)} %add_convert_fusion) | copy-start | bytes 589828
  99.3 7.5 %collective-permute-start.2 = (bf16[15,384]{1,0:T(8,128)(2,1)S(1)}, bf16[15,384]{1,0:T(8,128)(2,1)S(1)}, u32[]{:S(2)}, u32[]{:S(2)}) collective-permute-start(bf16[15,384]{1,0:T(8,128)(2,1)S(1)} %get-tuple-element.47), channel_id=1, source_target_pairs={{0,4},{4,8},{8,12},{12,16},{16,20},{20,24},{24,28},{28,32},{32,36}... | collective-permute-start | bytes 34568 | tf_op jit(solution)/shard_map/ppermute | solution.py:24
  103.7 5.0 %collective-permute-start.3 = (bf16[15,384]{1,0:T(8,128)(2,1)S(1)}, bf16[15,384]{1,0:T(8,128)(2,1)S(1)}, u32[]{:S(2)}, u32[]{:S(2)}) collective-permute-start(bf16[15,384]{1,0:T(8,128)(2,1)S(1)} %get-tuple-element.48), channel_id=1, source_target_pairs={{4,0},{8,4},{12,8},{16,12},{20,16},{24,20},{28,24},{32,28},{36,32}... | collective-permute-start | bytes 34568 | tf_op jit(solution)/shard_map/ppermute | solution.py:25
  114.1 5.6 %collective-permute-start.4 = (bf16[15,384]{1,0:T(8,128)(2,1)S(1)}, bf16[15,384]{1,0:T(8,128)(2,1)S(1)}, u32[]{:S(2)}, u32[]{:S(2)}) collective-permute-start(bf16[15,384]{1,0:T(8,128)(2,1)S(1)} %get-tuple-element.45), channel_id=1, source_target_pairs={{4,0},{8,4},{12,8},{16,12},{20,16},{24,20},{28,24},{32,28},{36,32}... | collective-permute-start | bytes 34568 | tf_op jit(solution)/shard_map/ppermute | solution.py:25
  116.1 4.5 %collective-permute-start.5 = (bf16[15,384]{1,0:T(8,128)(2,1)S(1)}, bf16[15,384]{1,0:T(8,128)(2,1)S(1)}, u32[]{:S(2)}, u32[]{:S(2)}) collective-permute-start(bf16[15,384]{1,0:T(8,128)(2,1)S(1)} %get-tuple-element.46), channel_id=1, source_target_pairs={{0,4},{4,8},{8,12},{12,16},{16,20},{20,24},{24,28},{28,32},{32,36}... | collective-permute-start | bytes 34568 | tf_op jit(solution)/shard_map/ppermute | solution.py:24
  132.8 6.4 %copy-start.7 = (bf16[768,1,384]{0,2,1:T(8,128)(2,1)S(1)}, bf16[768,1,384]{0,2,1:T(8,128)(2,1)}, u32[]{:S(2)}) copy-start(bf16[768,1,384]{0,2,1:T(8,128)(2,1)} %copy-done.6) | copy-start | bytes 1769476
  132.9 13.2 %collective-permute-start.6 = (f32[256,2,384]{0,2,1:T(8,128)S(1)}, f32[256,2,384]{0,2,1:T(8,128)S(1)}, u32[]{:S(2)}, u32[]{:S(2)}) collective-permute-start(f32[256,2,384]{0,2,1:T(8,128)S(1)} %get-tuple-element.40), channel_id=1, source_target_pairs={{0,4},{4,8},{8,12},{12,16},{16,20},{20,24},{24,28},{28,32},{32,36}... | collective-permute-start | bytes 2359304 | tf_op jit(solution)/shard_map/ppermute | solution.py:33
  137.3 13.3 %collective-permute-start.7 = (f32[256,2,384]{0,2,1:T(8,128)S(1)}, f32[256,2,384]{0,2,1:T(8,128)S(1)}, u32[]{:S(2)}, u32[]{:S(2)}) collective-permute-start(f32[256,2,384]{0,2,1:T(8,128)S(1)} %get-tuple-element.41), channel_id=1, source_target_pairs={{4,0},{8,4},{12,8},{16,12},{20,16},{24,20},{28,24},{32,28},{36,32}... | collective-permute-start | bytes 2359304 | tf_op jit(solution)/shard_map/ppermute | solution.py:33
  140.7 10.1 %copy-start.15 = (bf16[1536,384]{1,0:T(8,128)(2,1)S(1)}, bf16[1536,384]{1,0:T(8,128)(2,1)}, u32[]{:S(2)}) copy-start(bf16[1536,384]{1,0:T(8,128)(2,1)} %param.14) | copy-start | bytes 3538948
  153.8 76.2 %copy-start.2 = (bf16[256,1536]{1,0:T(8,128)(2,1)S(1)}, bf16[256,1536]{1,0:T(8,128)(2,1)}, u32[]{:S(2)}) copy-start(bf16[256,1536]{1,0:T(8,128)(2,1)} %copy-done.1) | copy-start | bytes 2359300
  153.8 76.2 %copy-start.24 = (f32[256]{0:T(256)S(1)}, f32[256]{0:T(256)}, u32[]{:S(2)}) copy-start(f32[256]{0:T(256)} %copy-done.23) | copy-start | bytes 3076
  153.8 76.2 %copy-start.26 = (f32[256]{0:T(256)S(1)}, f32[256]{0:T(256)}, u32[]{:S(2)}) copy-start(f32[256]{0:T(256)} %copy-done.25) | copy-start | bytes 3076
  153.9 76.2 %copy-start.28 = (f32[1536]{0:T(1024)S(1)}, f32[1536]{0:T(1024)}, u32[]{:S(2)}) copy-start(f32[1536]{0:T(1024)} %param.12) | copy-start | bytes 18436
  155.7 76.2 %copy-start.11 = (bf16[256,384]{1,0:T(8,128)(2,1)S(1)}, bf16[256,384]{1,0:T(8,128)(2,1)}, u32[]{:S(2)}) copy-start(bf16[256,384]{1,0:T(8,128)(2,1)} %fusion.41) | copy-start | bytes 589828
  (10 other events, 16.8 us)
Sparse Core Ops, SparseCore 0:
  154.0 75.9 all-reduce.2
where the time goes:
time: 240 us
  waiting for transfers between devices  111 us (46%)
  starting transfers between devices  47.4 us (20%)
  other arithmetic  23.8 us (10%)
  matrix products  16.9 us (7%)
  between operations  14.6 us (6%)
  blocking collectives  13.3 us (6%)
  local copies, waits for them, and re-layouts  13 us (5%)
    psum x1, waiting for transfers between devices, on_device(): grad_whole = lax.psum(grad_normed, 'head')  74.3 us
    all_to_all x1, waiting for transfers between devices, on_device(): lax.all_to_all(blocks, 'seq', split_axis=0, concat_axis=0, tiled=True)  20.6 us
    all_to_all x1, starting transfers between devices, on_device(): lax.all_to_all(blocks, 'seq', split_axis=0, concat_axis=0, tiled=True)  20.4 us
    all_gather x1, blocking collectives, on_device(): gathered = lax.all_gather(frame_part, 'head', axis=1, tiled=True)  13.3 us
    ppermute x3, starting transfers between devices, extended_2(): before = lax.ppermute(last, axis, up)  12.5 us
    ppermute x2, waiting for transfers between devices, from_behind(): return lax.ppermute(shard, axis, pairs)  9.9 us
    ppermute x3, starting transfers between devices, extended_2(): after = lax.ppermute(leading, axis, down)  8.18 us
    ppermute x2, starting transfers between devices, from_behind(): return lax.ppermute(shard, axis, pairs)  6.25 us
  transfers between devices with their start and end apart: 10, of which 8 were waited for; matrix products, arithmetic and copies ran while one was open for 4% of the time, Pallas kernels for 0%

commit v1 on v0

--- a/solution.py
+++ b/solution.py
@@ -53,7 +53,6 @@
     head_count = part_cols // HEAD_DIM
     frame_total = frames * seq_count
     capacity = loader_rows.shape[0] // seq_count
-    column_start = lax.axis_index("head") * part_cols
     score_scale = 1.0 / math.sqrt(HEAD_DIM)
     blocks = loader_rows.reshape(seq_count, capacity, part_cols)
     arrived = lax.all_to_all(blocks, "seq", split_axis=0, concat_axis=0, tiled=True)
@@ -153,11 +152,12 @@
         "hqk,qhe->khe", weights_low, upstream, preferred_element_type=jnp.float32
     ).reshape(span, part_cols)
     kv_grads = jnp.stack([grad_keys, grad_values], axis=1)
-    from_right = from_behind(kv_grads[:WIN], "seq", -1)
-    from_left = from_behind(kv_grads[frames + WIN :], "seq", 1)
+    kv_sent = kv_grads.astype(jnp.bfloat16)
+    from_right = from_behind(kv_sent[:WIN], "seq", -1)
+    from_left = from_behind(kv_sent[frames + WIN :], "seq", 1)
     own_grads = kv_grads[WIN : WIN + frames]
-    own_grads = own_grads + from_left
-    own_grads = own_grads + from_right
+    own_grads = own_grads + from_left.astype(jnp.float32)
+    own_grads = own_grads + from_right.astype(jnp.float32)
     grad_key_low = own_grads[:, 0].astype(jnp.bfloat16)
     grad_value_low = own_grads[:, 1].astype(jnp.bfloat16)
     grad_normed = (
@@ -165,12 +165,20 @@
         + back_project(grad_key_low, wk)
         + back_project(grad_value_low, wv)
     )
-    grad_whole = lax.psum(grad_normed, "head")
-    scaled = grad_whole * gain[None, :]
-    mean_term = jnp.mean(scaled, axis=1, keepdims=True)
-    slope_term = jnp.mean(scaled * unit_rows, axis=1, keepdims=True)
-    through_all = inverse_std * (scaled - mean_term - unit_rows * slope_term)
-    through = lax.dynamic_slice_in_dim(through_all, column_start, part_cols, 1)
+    parts = lax.axis_size("head")
+    scaled_part = grad_normed * gain[None, :]
+    sums = jnp.stack([jnp.sum(scaled_part, axis=1), jnp.sum(scaled_part * unit_rows, axis=1)])
+    sums_all = lax.all_to_all(
+        jnp.broadcast_to(sums[None], (parts,) + sums.shape), "head", split_axis=0, concat_axis=0, tiled=True
+    )
+    means = jnp.sum(sums_all, axis=0) / scaled_part.shape[1]
+    chunks = jnp.transpose(
+        scaled_part.astype(jnp.bfloat16).reshape(frames, parts, part_cols), (1, 0, 2)
+    )
+    arrived_parts = lax.all_to_all(chunks, "head", split_axis=0, concat_axis=0, tiled=True)
+    scaled = jnp.sum(arrived_parts.astype(jnp.float32), axis=0)
+    unit_part = (frame_part.astype(jnp.float32) - row_mean) * inverse_std
+    through = inverse_std * (scaled - means[0][:, None] - unit_part * means[1][:, None])
     grad_input = (grad_residual.astype(jnp.float32) + through).astype(jnp.bfloat16)
     return (output, grad_input)
 

time: 240 us -> 178 us (0.74)
  the two profiles are of different devices: /device:TPU:1 before, /device:TPU:103 now
where the time goes in v1:
time: 178 us; the launch traced here: 177 us
  starting transfers between devices  62.8 us (35%)
  waiting for transfers between devices  48.5 us (27%)
  other arithmetic  22 us (12%)
  matrix products  16.1 us (9%)
  local copies, waits for them, and re-layouts  13.4 us (8%)
  blocking collectives  13.2 us (7%)
    all_to_all x1, waiting for transfers between devices, on_device(): lax.all_to_all(blocks, 'seq', split_axis=0, concat_axis=0, tiled=True)  19.6 us
    ppermute x3, starting transfers between devices, extended_2(): before = lax.ppermute(last, axis, up)  19.4 us
    all_to_all x1, starting transfers between devices, on_device(): lax.all_to_all(blocks, 'seq', split_axis=0, concat_axis=0, tiled=True)  18.4 us
    all_gather x1, blocking collectives, on_device(): gathered = lax.all_gather(frame_part, 'head', axis=1, tiled=True)  13.2 us
    ppermute x2, starting transfers between devices, from_behind(): return lax.ppermute(shard, axis, pairs)  9.7 us
    ppermute x2, waiting for transfers between devices, from_behind(): return lax.ppermute(shard, axis, pairs)  9 us
    ppermute x3, starting transfers between devices, extended_2(): after = lax.ppermute(leading, axis, down)  8.15 us
    all_to_all x1, waiting for transfers between devices, on_device(): lax.all_to_all(chunks, 'head', split_axis=0, concat_axis=0, tiled=True)  7.44 us
  transfers between devices with their start and end apart: 11, of which 9 were waited for; matrix products, arithmetic and copies ran while one was open for 6% of the time, Pallas kernels for 0%

profile of v1, /device:TPU:103, one launch (start us, length us, event | category | flops | bytes accessed | tf_op | source)
XLA Modules:
  0.0 177.3 jit_solution(11795281395333560653)
XLA Ops:
  0.7 1.9 %reshape.223 = bf16[128,4,384]{2,1,0:T(4,128)(2,1)} reshape(bf16[512,384]{1,0:T(8,128)(2,1)} %param.9) | data formatting | bytes 786432 | tf_op jit(solution)/shard_map/reshape | solution.py:57
  2.6 18.4 %all-to-all-start = ((bf16[128,4,384]{2,1,0:T(4,128)(2,1)}), bf16[128,4,384]{2,1,0:T(4,128)(2,1)S(1)}, u32[]{:S(2)}, u32[]{:S(2)}) async-start(bf16[128,4,384]{2,1,0:T(4,128)(2,1)} %reshape.223), calls=%async_computation | async-start | bytes 786432 | tf_op jit(solution)/shard_map/all_to_all | solution.py:58
  25.8 19.6 %all-to-all-done = bf16[128,4,384]{2,1,0:T(4,128)(2,1)S(1)} async-done(((bf16[128,4,384]{2,1,0:T(4,128)(2,1)}), bf16[128,4,384]{2,1,0:T(4,128)(2,1)S(1)}, u32[]{:S(2)}, u32[]{:S(2)}) %all-to-all-start) | async-done | bytes 393248 | tf_op jit(solution)/shard_map/all_to_all | solution.py:58
  45.5 1.2 gather_fusion
  46.8 13.2 %all_gather.3 = bf16[256,1536]{1,0:T(8,128)(2,1)S(1)} all-gather(bf16[256,384]{1,0:T(8,128)(2,1)S(1)} %broadcast_select_fusion), channel_id=1, replica_groups=mesh['seq'=128,'head'=4] {'head'}, dimensions={1}, use_global_device_ids=true | all-gather | bytes 983040 | tf_op jit(solution)/shard_map/all_gather | solution.py:67
  62.6 4.1 %collective-permute-start.1 = (bf16[256,2,384]{2,0,1:T(8,128)(2,1)S(1)}, bf16[256,2,384]{2,0,1:T(8,128)(2,1)S(1)}, u32[]{:S(2)}, u32[]{:S(2)}) collective-permute-start(bf16[256,2,384]{2,0,1:T(8,128)(2,1)S(1)} %pad_maximum_fusion.2), channel_id=1, source_target_pairs={{4,0},{8,4},{12,8},{16,12},{20,16},{24,20},{28,24},{32,28},{36,32}... | collective-permute-start | bytes 1179656 | tf_op jit(solution)/shard_map/ppermute | solution.py:25
  66.8 4.8 %collective-permute-start = (bf16[256,2,384]{2,0,1:T(8,128)(2,1)S(1)}, bf16[256,2,384]{2,0,1:T(8,128)(2,1)S(1)}, u32[]{:S(2)}, u32[]{:S(2)}) collective-permute-start(bf16[256,2,384]{2,0,1:T(8,128)(2,1)S(1)} %pad_maximum_fusion.2), channel_id=1, source_target_pairs={{0,4},{4,8},{8,12},{12,16},{16,20},{20,24},{24,28},{28,32},{32,36}... | collective-permute-start | bytes 1179656 | tf_op jit(solution)/shard_map/ppermute | solution.py:24
  73.0 2.0 %collective-permute-done.1 = bf16[256,2,384]{2,0,1:T(8,128)(2,1)S(1)} collective-permute-done((bf16[256,2,384]{2,0,1:T(8,128)(2,1)S(1)}, bf16[256,2,384]{2,0,1:T(8,128)(2,1)S(1)}, u32[]{:S(2)}, u32[]{:S(2)}) %collective-permute-start.1) | collective-permute-done | bytes 393248 | tf_op jit(solution)/shard_map/ppermute | solution.py:25
  75.1 1.2 collective-permute-done
  77.9 4.4 %fusion.124 = (f32[6,256]{1,0:T(8,128)}, f32[6,256,768]{2,1,0:T(8,128)}) fusion(pred[256,768]{1,0:T(8,128)(4,1)S(1)} %fusion.24, bf16[256,6,64]{0,2,1:T(8,128)(2,1)S(1)} %bitcast.84, bf16[768,6,64]{0,2,1:T(8,128)(2,1)S(1)} %bitcast.79), kind=kOutput, calls=%fused_computation.327 | convolution fusion | flops 155714304 | bytes 5707776 | tf_op jit(solution)/shard_map/sub | solution.py:96
  82.3 2.8 %fusion.7 = bf16[6,256,768]{2,1,0:T(8,128)(2,1)S(1)} fusion(f32[6,256,768]{2,1,0:T(8,128)} %get-tuple-element.81, f32[6,256]{1,0:T(8,128)} %get-tuple-element.80), kind=kLoop, calls=%fused_computation.19 | loop fusion | flops 2359296 | bytes 7084032 | tf_op jit(solution)/shard_map/convert_element_type | solution.py:99
  85.1 1.6 fusion.125
  86.7 1.9 %copy.39 = f32[256,384]{1,0:T(8,128)} copy(f32[256,384]{0,1:T(8,128)} %bitcast.76) | data formatting | bytes 786432 | tf_op jit(solution)/shard_map/reshape | solution.py:103
  88.6 1.2 fusion.27
  89.9 7.7 %collective-permute-start.2 = (bf16[15,384]{1,0:T(8,128)(2,1)S(1)}, bf16[15,384]{1,0:T(8,128)(2,1)S(1)}, u32[]{:S(2)}, u32[]{:S(2)}) collective-permute-start(bf16[15,384]{1,0:T(8,128)(2,1)S(1)} %get-tuple-element.46), channel_id=1, source_target_pairs={{0,4},{4,8},{8,12},{12,16},{16,20},{20,24},{24,28},{28,32},{32,36}... | collective-permute-start | bytes 34568 | tf_op jit(solution)/shard_map/ppermute | solution.py:24
  97.6 2.1 %collective-permute-start.3 = (bf16[15,384]{1,0:T(8,128)(2,1)S(1)}, bf16[15,384]{1,0:T(8,128)(2,1)S(1)}, u32[]{:S(2)}, u32[]{:S(2)}) collective-permute-start(bf16[15,384]{1,0:T(8,128)(2,1)S(1)} %get-tuple-element.47), channel_id=1, source_target_pairs={{4,0},{8,4},{12,8},{16,12},{20,16},{24,20},{28,24},{32,28},{36,32}... | collective-permute-start | bytes 34568 | tf_op jit(solution)/shard_map/ppermute | solution.py:25
  100.8 5.2 %collective-permute-done.3 = bf16[15,384]{1,0:T(8,128)(2,1)S(1)} collective-permute-done((bf16[15,384]{1,0:T(8,128)(2,1)S(1)}, bf16[15,384]{1,0:T(8,128)(2,1)S(1)}, u32[]{:S(2)}, u32[]{:S(2)}) %collective-permute-start.3) | collective-permute-done | bytes 11552 | tf_op jit(solution)/shard_map/ppermute | solution.py:25
  105.9 5.4 %fusion.52 = (bf16[256,384]{1,0:T(8,128)(2,1)S(1)}, f32[256,384]{1,0:T(8,128)}) fusion(bf16[256,384]{1,0:T(8,128)(2,1)} %param.17, f32[384]{0:T(512)S(1)} %get-tuple-element.33, bf16[15,384]{1,0:T(8,128)(2,1)S(1)} %collective-permute-done.3, bf16[256,384]{1,0:T(8,128)(2,1)S(1)} %fusion.27, pred[256]{0:T(512)(128)(4,1)} %get-tuple-element.49, ...), kind=kLoop, calls=%fused_computation.134 | loop fusion | flops 21823488 | bytes 1061376 | tf_op jit(solution)/shard_map/convert_element_type | solution.py:120
  111.3 1.9 %collective-permute-start.4 = (bf16[15,384]{1,0:T(8,128)(2,1)S(1)}, bf16[15,384]{1,0:T(8,128)(2,1)S(1)}, u32[]{:S(2)}, u32[]{:S(2)}) collective-permute-start(bf16[15,384]{1,0:T(8,128)(2,1)S(1)} %get-tuple-element.44), channel_id=1, source_target_pairs={{4,0},{8,4},{12,8},{16,12},{20,16},{24,20},{28,24},{32,28},{36,32}... | collective-permute-start | bytes 34568 | tf_op jit(solution)/shard_map/ppermute | solution.py:25
  113.3 7.0 %collective-permute-start.5 = (bf16[15,384]{1,0:T(8,128)(2,1)S(1)}, bf16[15,384]{1,0:T(8,128)(2,1)S(1)}, u32[]{:S(2)}, u32[]{:S(2)}) collective-permute-start(bf16[15,384]{1,0:T(8,128)(2,1)S(1)} %get-tuple-element.45), channel_id=1, source_target_pairs={{0,4},{4,8},{8,12},{12,16},{16,20},{20,24},{24,28},{28,32},{32,36}... | collective-permute-start | bytes 34568 | tf_op jit(solution)/shard_map/ppermute | solution.py:24
  121.1 5.2 %fusion.53 = bf16[256,384]{1,0:T(8,128)(2,1)} fusion(bf16[256,384]{1,0:T(8,128)(2,1)S(1)} %copy-done.21, bf16[256,384]{1,0:T(8,128)(2,1)S(1)} %get-tuple-element.35, bf16[15,384]{1,0:T(8,128)(2,1)S(1)} %collective-permute-done.5, bf16[15,384]{1,0:T(8,128)(2,1)S(1)} %collective-permute-done.4, f32[384]{0:T(512)S(1)} %get-tuple-element.33, ...), kind=kLoop, calls=%fused_computation.135 | loop fusion | flops 21135360 | bytes 668160 | tf_op jit(solution)/shard_map/convert_element_type | solution.py:134
  126.3 1.7 copy.40
  128.0 1.6 fusion.128
  129.7 3.0 %multiply_convert_fusion = bf16[6,256,768]{2,1,0:T(8,128)(2,1)S(1)} fusion(f32[6,256]{1,0:T(8,128)S(1)} %bitcast.89, bf16[256,6,64]{0,2,1:T(8,128)(2,1)S(1)} %bitcast.83, bf16[768,6,64]{0,2,1:T(8,128)(2,1)S(1)} %bitcast.78, f32[6,256,768]{2,1,0:T(8,128)} %get-tuple-element.81, f32[6,256]{1,0:T(8,128)S(1)} %copy-done.28), kind=kOutput, calls=%fused_computation.2 | convolution fusion | flops 156893184 | bytes 7876608 | tf_op jit(solution)/shard_map/qhe,khe->hqk/dot_general | solution.py:137
  133.6 7.6 %collective-permute-start.6 = (bf16[256,2,384]{0,2,1:T(8,128)(2,1)S(1)}, bf16[256,2,384]{0,2,1:T(8,128)(2,1)S(1)}, u32[]{:S(2)}, u32[]{:S(2)}) collective-permute-start(bf16[256,2,384]{0,2,1:T(8,128)(2,1)S(1)} %get-tuple-element.40), channel_id=1, source_target_pairs={{0,4},{4,8},{8,12},{12,16},{16,20},{20,24},{24,28},{28,32},{32,36}... | collective-permute-start | bytes 1179656 | tf_op jit(solution)/shard_map/ppermute | solution.py:33
  141.2 2.1 %collective-permute-start.7 = (bf16[256,2,384]{0,2,1:T(8,128)(2,1)S(1)}, bf16[256,2,384]{0,2,1:T(8,128)(2,1)S(1)}, u32[]{:S(2)}, u32[]{:S(2)}) collective-permute-start(bf16[256,2,384]{0,2,1:T(8,128)(2,1)S(1)} %get-tuple-element.41), channel_id=1, source_target_pairs={{4,0},{8,4},{12,8},{16,12},{20,16},{24,20},{28,24},{32,28},{36,32}... | collective-permute-start | bytes 1179656 | tf_op jit(solution)/shard_map/ppermute | solution.py:33
  144.8 1.1 collective-permute-done.6
  145.9 7.9 %collective-permute-done.7 = bf16[256,2,384]{0,2,1:T(8,128)(2,1)S(1)} collective-permute-done((bf16[256,2,384]{0,2,1:T(8,128)(2,1)S(1)}, bf16[256,2,384]{0,2,1:T(8,128)(2,1)S(1)}, u32[]{:S(2)}, u32[]{:S(2)}) %collective-permute-start.7) | collective-permute-done | bytes 393248 | tf_op jit(solution)/shard_map/ppermute | solution.py:33
  156.7 3.5 %all-to-all-start.2 = ((f32[4,2,256]{2,1,0:T(2,128)}), f32[4,2,256]{2,1,0:T(2,128)S(1)}, u32[]{:S(2)}, u32[]{:S(2)}) async-start(f32[4,2,256]{2,1,0:T(2,128)} %broadcast_in_dim.479), calls=%async_computation.2 | async-start | bytes 16384 | tf_op jit(solution)/shard_map/all_to_all | solution.py:171
  161.1 3.2 %all-to-all-done.2 = f32[4,2,256]{2,1,0:T(2,128)S(1)} async-done(((f32[4,2,256]{2,1,0:T(2,128)}), f32[4,2,256]{2,1,0:T(2,128)S(1)}, u32[]{:S(2)}, u32[]{:S(2)}) %all-to-all-start.2) | async-done | bytes 8224 | tf_op jit(solution)/shard_map/all_to_all | solution.py:171
  164.3 3.6 %all-to-all-start.1 = ((bf16[4,256,384]{2,1,0:T(8,128)(2,1)}), bf16[4,256,384]{2,1,0:T(8,128)(2,1)S(1)}, u32[]{:S(2)}, u32[]{:S(2)}) async-start(bf16[4,256,384]{2,1,0:T(8,128)(2,1)} %bitcast.70), calls=%async_computation.1 | async-start | bytes 1572864 | tf_op jit(solution)/shard_map/all_to_all | solution.py:178
  168.8 7.4 %all-to-all-done.1 = bf16[4,256,384]{2,1,0:T(8,128)(2,1)S(1)} async-done(((bf16[4,256,384]{2,1,0:T(8,128)(2,1)}), bf16[4,256,384]{2,1,0:T(8,128)(2,1)S(1)}, u32[]{:S(2)}, u32[]{:S(2)}) %all-to-all-start.1) | async-done | bytes 786464 | tf_op jit(solution)/shard_map/all_to_all | solution.py:178
  (133 shorter events, 20.4 us)
Async XLA Ops:
  0.6 60.0 %copy-start = (bf16[1536,384]{1,0:T(8,128)(2,1)S(1)}, bf16[1536,384]{1,0:T(8,128)(2,1)}, u32[]{:S(2)}) copy-start(bf16[1536,384]{1,0:T(8,128)(2,1)} %param.15) | copy-start | bytes 3538948
  0.6 20.4 %copy-start.31 = (s32[170]{0:T(256)S(1)}, s32[170]{0:T(256)}, u32[]{:S(2)}) copy-start(s32[170]{0:T(256)} %param.11) | copy-start | bytes 2044
  0.7 21.2 %copy-start.22 = (s32[128,128]{1,0:T(8,128)S(1)}, s32[128,128]{1,0:T(8,128)}, u32[]{:S(2)}) copy-start(s32[128,128]{1,0:T(8,128)} %param.10) | copy-start | bytes 196612
  2.6 42.8 %all-to-all-start = ((bf16[128,4,384]{2,1,0:T(4,128)(2,1)}), bf16[128,4,384]{2,1,0:T(4,128)(2,1)S(1)}, u32[]{:S(2)}, u32[]{:S(2)}) async-start(bf16[128,4,384]{2,1,0:T(4,128)(2,1)} %reshape.223), calls=%async_computation | async-start | bytes 786432 | tf_op jit(solution)/shard_map/all_to_all | solution.py:58
  22.7 24.2 %copy-start.26 = (pred[256]{0:T(512)(128)(4,1)}, pred[256]{0:T(512)(128)(4,1)S(1)}, u32[]{:S(2)}) copy-start(pred[256]{0:T(512)(128)(4,1)S(1)} %compare_and_fusion) | copy-start | bytes 772
  46.7 14.6 %copy-start.4 = (bf16[256,384]{1,0:T(8,128)(2,1)}, bf16[256,384]{1,0:T(8,128)(2,1)S(1)}, u32[]{:S(2)}) copy-start(bf16[256,384]{1,0:T(8,128)(2,1)S(1)} %gather_fusion) | copy-start | bytes 589828
  46.7 13.9 %copy-start.32 = (f32[1536]{0:T(1024)S(1)}, f32[1536]{0:T(1024)}, u32[]{:S(2)}) copy-start(f32[1536]{0:T(1024)} %param.12) | copy-start | bytes 18436
  60.1 12.2 %copy-start.1 = (bf16[256,1536]{1,0:T(8,128)(2,1)}, bf16[256,1536]{1,0:T(8,128)(2,1)S(1)}, u32[]{:S(2)}) copy-start(bf16[256,1536]{1,0:T(8,128)(2,1)S(1)} %all_gather.3) | copy-start | bytes 2359300
  60.3 12.0 %copy-start.24 = (f32[256]{0:T(256)}, f32[256]{0:T(256)S(1)}, u32[]{:S(2)}) copy-start(f32[256]{0:T(256)S(1)} %broadcast_multiply_fusion.1) | copy-start | bytes 3076
  60.7 11.6 %copy-start.29 = (f32[256]{0:T(256)}, f32[256]{0:T(256)S(1)}, u32[]{:S(2)}) copy-start(f32[256]{0:T(256)S(1)} %add_rsqrt_fusion) | copy-start | bytes 3076
  61.9 9.6 %copy-start.23 = (f32[31,384]{1,0:T(8,128)S(1)}, f32[31,384]{1,0:T(8,128)}, u32[]{:S(2)}) copy-start(f32[31,384]{1,0:T(8,128)} %param.16) | copy-start | bytes 142852
  61.9 10.3 %copy-start.15 = (bf16[1536,384]{1,0:T(8,128)(2,1)S(1)}, bf16[1536,384]{1,0:T(8,128)(2,1)}, u32[]{:S(2)}) copy-start(bf16[1536,384]{1,0:T(8,128)(2,1)} %param.13) | copy-start | bytes 3538948
  62.6 12.4 %collective-permute-start.1 = (bf16[256,2,384]{2,0,1:T(8,128)(2,1)S(1)}, bf16[256,2,384]{2,0,1:T(8,128)(2,1)S(1)}, u32[]{:S(2)}, u32[]{:S(2)}) collective-permute-start(bf16[256,2,384]{2,0,1:T(8,128)(2,1)S(1)} %pad_maximum_fusion.2), channel_id=1, source_target_pairs={{4,0},{8,4},{12,8},{16,12},{20,16},{24,20},{28,24},{32,28},{36,32}... | collective-permute-start | bytes 1179656 | tf_op jit(solution)/shard_map/ppermute | solution.py:25
  66.8 9.5 %collective-permute-start = (bf16[256,2,384]{2,0,1:T(8,128)(2,1)S(1)}, bf16[256,2,384]{2,0,1:T(8,128)(2,1)S(1)}, u32[]{:S(2)}, u32[]{:S(2)}) collective-permute-start(bf16[256,2,384]{2,0,1:T(8,128)(2,1)S(1)} %pad_maximum_fusion.2), channel_id=1, source_target_pairs={{0,4},{4,8},{8,12},{12,16},{16,20},{20,24},{24,28},{28,32},{32,36}... | collective-permute-start | bytes 1179656 | tf_op jit(solution)/shard_map/ppermute | solution.py:24
  76.7 5.6 %copy-start.8 = (bf16[768,1,384]{0,2,1:T(8,128)(2,1)}, bf16[768,1,384]{0,2,1:T(8,128)(2,1)S(1)}, u32[]{:S(2)}) copy-start(bf16[768,1,384]{0,2,1:T(8,128)(2,1)S(1)} %copy.38) | copy-start | bytes 1769476
  88.6 32.5 %copy-start.21 = (bf16[256,384]{1,0:T(8,128)(2,1)S(1)}, bf16[256,384]{1,0:T(8,128)(2,1)}, u32[]{:S(2)}) copy-start(bf16[256,384]{1,0:T(8,128)(2,1)} %param.17) | copy-start | bytes 589828
  89.9 16.1 %copy-start.10 = (bf16[256,384]{1,0:T(8,128)(2,1)}, bf16[256,384]{1,0:T(8,128)(2,1)S(1)}, u32[]{:S(2)}) copy-start(bf16[256,384]{1,0:T(8,128)(2,1)S(1)} %fusion.27) | copy-start | bytes 589828
  89.9 10.9 %collective-permute-start.2 = (bf16[15,384]{1,0:T(8,128)(2,1)S(1)}, bf16[15,384]{1,0:T(8,128)(2,1)S(1)}, u32[]{:S(2)}, u32[]{:S(2)}) collective-permute-start(bf16[15,384]{1,0:T(8,128)(2,1)S(1)} %get-tuple-element.46), channel_id=1, source_target_pairs={{0,4},{4,8},{8,12},{12,16},{16,20},{20,24},{24,28},{28,32},{32,36}... | collective-permute-start | bytes 34568 | tf_op jit(solution)/shard_map/ppermute | solution.py:24
  97.6 8.3 %collective-permute-start.3 = (bf16[15,384]{1,0:T(8,128)(2,1)S(1)}, bf16[15,384]{1,0:T(8,128)(2,1)S(1)}, u32[]{:S(2)}, u32[]{:S(2)}) collective-permute-start(bf16[15,384]{1,0:T(8,128)(2,1)S(1)} %get-tuple-element.47), channel_id=1, source_target_pairs={{4,0},{8,4},{12,8},{16,12},{20,16},{24,20},{28,24},{32,28},{36,32}... | collective-permute-start | bytes 34568 | tf_op jit(solution)/shard_map/ppermute | solution.py:25
  111.3 8.9 %collective-permute-start.4 = (bf16[15,384]{1,0:T(8,128)(2,1)S(1)}, bf16[15,384]{1,0:T(8,128)(2,1)S(1)}, u32[]{:S(2)}, u32[]{:S(2)}) collective-permute-start(bf16[15,384]{1,0:T(8,128)(2,1)S(1)} %get-tuple-element.44), channel_id=1, source_target_pairs={{4,0},{8,4},{12,8},{16,12},{20,16},{24,20},{28,24},{32,28},{36,32}... | collective-permute-start | bytes 34568 | tf_op jit(solution)/shard_map/ppermute | solution.py:25
  113.3 7.8 %collective-permute-start.5 = (bf16[15,384]{1,0:T(8,128)(2,1)S(1)}, bf16[15,384]{1,0:T(8,128)(2,1)S(1)}, u32[]{:S(2)}, u32[]{:S(2)}) collective-permute-start(bf16[15,384]{1,0:T(8,128)(2,1)S(1)} %get-tuple-element.45), channel_id=1, source_target_pairs={{0,4},{4,8},{8,12},{12,16},{16,20},{20,24},{24,28},{28,32},{32,36}... | collective-permute-start | bytes 34568 | tf_op jit(solution)/shard_map/ppermute | solution.py:24
  133.5 9.8 %copy-start.9 = (bf16[768,1,384]{0,2,1:T(8,128)(2,1)S(1)}, bf16[768,1,384]{0,2,1:T(8,128)(2,1)}, u32[]{:S(2)}) copy-start(bf16[768,1,384]{0,2,1:T(8,128)(2,1)} %copy-done.8) | copy-start | bytes 1769476
  133.6 12.4 %collective-permute-start.6 = (bf16[256,2,384]{0,2,1:T(8,128)(2,1)S(1)}, bf16[256,2,384]{0,2,1:T(8,128)(2,1)S(1)}, u32[]{:S(2)}, u32[]{:S(2)}) collective-permute-start(bf16[256,2,384]{0,2,1:T(8,128)(2,1)S(1)} %get-tuple-element.40), channel_id=1, source_target_pairs={{0,4},{4,8},{8,12},{12,16},{16,20},{20,24},{24,28},{28,32},{32,36}... | collective-permute-start | bytes 1179656 | tf_op jit(solution)/shard_map/ppermute | solution.py:33
  141.2 12.5 %collective-permute-start.7 = (bf16[256,2,384]{0,2,1:T(8,128)(2,1)S(1)}, bf16[256,2,384]{0,2,1:T(8,128)(2,1)S(1)}, u32[]{:S(2)}, u32[]{:S(2)}) collective-permute-start(bf16[256,2,384]{0,2,1:T(8,128)(2,1)S(1)} %get-tuple-element.41), channel_id=1, source_target_pairs={{4,0},{8,4},{12,8},{16,12},{20,16},{24,20},{28,24},{32,28},{36,32}... | collective-permute-start | bytes 1179656 | tf_op jit(solution)/shard_map/ppermute | solution.py:33
  144.8 9.2 %copy-start.18 = (bf16[1536,384]{1,0:T(8,128)(2,1)S(1)}, bf16[1536,384]{1,0:T(8,128)(2,1)}, u32[]{:S(2)}) copy-start(bf16[1536,384]{1,0:T(8,128)(2,1)} %param.14) | copy-start | bytes 3538948
  156.7 7.6 %all-to-all-start.2 = ((f32[4,2,256]{2,1,0:T(2,128)}), f32[4,2,256]{2,1,0:T(2,128)S(1)}, u32[]{:S(2)}, u32[]{:S(2)}) async-start(f32[4,2,256]{2,1,0:T(2,128)} %broadcast_in_dim.479), calls=%async_computation.2 | async-start | bytes 16384 | tf_op jit(solution)/shard_map/all_to_all | solution.py:171
  160.2 7.8 %copy-start.11 = (bf16[256,384]{1,0:T(8,128)(2,1)S(1)}, bf16[256,384]{1,0:T(8,128)(2,1)}, u32[]{:S(2)}) copy-start(bf16[256,384]{1,0:T(8,128)(2,1)} %copy-done.10) | copy-start | bytes 589828
  160.2 7.8 %copy-start.14 = (f32[256,384]{1,0:T(8,128)S(1)}, f32[256,384]{1,0:T(8,128)}, u32[]{:S(2)}) copy-start(f32[256,384]{1,0:T(8,128)} %get-tuple-element.36) | copy-start | bytes 1179652
  164.3 12.0 %copy-start.5 = (bf16[256,384]{1,0:T(8,128)(2,1)S(1)}, bf16[256,384]{1,0:T(8,128)(2,1)}, u32[]{:S(2)}) copy-start(bf16[256,384]{1,0:T(8,128)(2,1)} %copy-done.4) | copy-start | bytes 589828
  164.3 12.1 %copy-start.13 = (bf16[256,384]{1,0:T(8,128)(2,1)S(1)}, bf16[256,384]{1,0:T(8,128)(2,1)}, u32[]{:S(2)}) copy-start(bf16[256,384]{1,0:T(8,128)(2,1)} %fusion.53) | copy-start | bytes 589828
  164.3 12.1 %copy-start.27 = (pred[256]{0:T(512)(128)(4,1)S(1)}, pred[256]{0:T(512)(128)(4,1)}, u32[]{:S(2)}) copy-start(pred[256]{0:T(512)(128)(4,1)} %copy-done.26) | copy-start | bytes 772
  164.3 11.9 %all-to-all-start.1 = ((bf16[4,256,384]{2,1,0:T(8,128)(2,1)}), bf16[4,256,384]{2,1,0:T(8,128)(2,1)S(1)}, u32[]{:S(2)}, u32[]{:S(2)}) async-start(bf16[4,256,384]{2,1,0:T(8,128)(2,1)} %bitcast.70), calls=%async_computation.1 | async-start | bytes 1572864 | tf_op jit(solution)/shard_map/all_to_all | solution.py:178
  (13 other events, 25.8 us)

commit v2 on v0

v2 whole, which is shorter than its diff:
```python
import math

import jax
import jax.numpy as jnp
from jax import lax
from jax.experimental import pallas as pl
from jax.experimental.pallas import tpu as pltpu
from jax.sharding import PartitionSpec as P

HEAD_DIM = 64
KS = 31
HALF_K = 15
WIN = 256
F = 256
PART = 384
GROUPS = 3
LANES = 128
HEADS_ALL = 4
CHUNK = 64
PAD = 16


EPSILON = 1e-05
MESH = pl.DeviceIdType.MESH


def segment_ids(positions, lengths, frame_total):
    utter_ends = jnp.cumsum(lengths)
    inside = (positions >= 0) & (positions < frame_total)
    counted = jnp.sum((utter_ends[None, :] <= positions[:, None]).astype(jnp.int32), axis=1)
    return jnp.where(inside, counted, -1)


def mm(a, b):
    return jnp.dot(a, b, preferred_element_type=jnp.float32)


def mm_nt(a, b):
    return lax.dot_general(a, b, (((1,), (1,)), ((), ())), preferred_element_type=jnp.float32)


def mm_tn(a, b):
    return lax.dot_general(a, b, (((0,), (0,)), ((), ())), preferred_element_type=jnp.float32)


def block_kernel(
    frame_ref, seg_row, seg_col, gain_ref, cw_ref, cot_ref, wq_hbm, wk_hbm, wv_hbm,
    out_ref, grad_ref,
    gath, unit, normed, inv_ref, wq, wk, wv, kv, qs, bias, wts, wlow, att,
    res_low, res_ext, res_halo, gc_low, gc_ext, gc_halo, gres,
    dq_ref, dsend, drecv, down, dkb, dvb, pacc, psend, precv, ssend, srecv,
    w_sem, ag_send, ag_recv, kv_send, kv_recv, rh_send, rh_recv, gh_send, gh_recv,
    d_send, d_recv, p_send, p_recv, s_send, s_recv,
):
    seq_count = lax.axis_size("seq")
    me = lax.axis_index("head")
    seq = lax.axis_index("seq")
    right = lax.rem(seq + 1, seq_count)
    left = lax.rem(seq + seq_count - 1, seq_count)
    scale = 1.0 / math.sqrt(HEAD_DIM)
    f32, bf16 = jnp.float32, jnp.bfloat16

    def peer(off):
        return lax.rem(me + off, HEADS_ALL)

    def remote(src, dst, send, recv, where):
        return pltpu.make_async_remote_copy(
            src_ref=src, dst_ref=dst, send_sem=send, recv_sem=recv, device_id=where, device_id_type=MESH
        )

    loads = [
        pltpu.make_async_copy(src, dst, w_sem.at[i])
        for i, (src, dst) in enumerate(((wk_hbm, wk), (wv_hbm, wv), (wq_hbm, wq)))
    ]
    for copy in loads:
        copy.start()

    barrier = pltpu.get_barrier_semaphore()
    for off in (1, 2, 3):
        pl.semaphore_signal(barrier, inc=1, device_id={"head": peer(off)}, device_id_type=MESH)
    for side in (left, right):
        pl.semaphore_signal(barrier, inc=1, device_id={"seq": side}, device_id_type=MESH)
    pl.semaphore_wait(barrier, 5)

    gathers = [
        remote(frame_ref, gath.at[me], ag_send.at[off - 1], ag_recv.at[off - 1], {"head": peer(off)})
        for off in (2, 1, 3)
    ]
    for copy in gathers:
        copy.start()
    gath[me] = frame_ref[...]

    rows_i = lax.broadcasted_iota(jnp.int32, (F, F), 0)
    cols_i = lax.broadcasted_iota(jnp.int32, (F, F), 1)
    own_seg = seg_col[WIN : WIN + F, 0:1]
    for b in range(3):
        ok = seg_row[:, b * F : (b + 1) * F] == own_seg
        if b == 0:
            ok = ok & (cols_i >= rows_i)
        if b == 2:
            ok = ok & (cols_i < rows_i)
        bias[b] = jnp.where(ok, 0.0, -jnp.inf)

    lane = lax.broadcasted_iota(jnp.int32, (1, LANES), 1)
    mf = [(lane < HEAD_DIM).astype(f32), (lane >= HEAD_DIM).astype(f32)]
    mb = [m.astype(bf16) for m in mf]

    for copy in gathers:
        copy.wait_recv()

    def norm_rows(r, carry):
        rows = pl.ds(pl.multiple_of(r * 32, 32), 32)
        xs = [gath[h, rows, :].astype(f32) for h in range(HEADS_ALL)]
        total = sum(jnp.sum(x, axis=1, keepdims=True) for x in xs)
        mean = total * (1.0 / (HEADS_ALL * PART))
        xs = [x - mean for x in xs]
        square = sum(jnp.sum(x * x, axis=1, keepdims=True) for x in xs)
        inv = lax.rsqrt(square * (1.0 / (HEADS_ALL * PART)) + EPSILON)
        inv_ref[rows, :] = jnp.broadcast_to(inv, (32, LANES))
        for h in range(HEADS_ALL):
            u = xs[h] * inv
            unit[h, rows, :] = u
            normed[rows, h * PART : (h + 1) * PART] = (u * gain_ref[h]).astype(bf16)
        return carry

    lax.fori_loop(0, F // 32, norm_rows, 0)

    halos = []
    for which, weight in ((0, wk), (1, wv)):
        loads[which].wait()
        rows = mm(normed[...], weight[...]).astype(bf16)
        for g in range(GROUPS):
            kv[1, which, g] = rows[:, g * LANES : (g + 1) * LANES]
        halos.append(
            remote(kv.at[1, which], kv.at[2, which], kv_send.at[which, 0], kv_recv.at[which, 0], {"seq": left})
        )
        halos.append(
            remote(kv.at[1, which], kv.at[0, which], kv_send.at[which, 1], kv_recv.at[which, 1], {"seq": right})
        )
        halos[-2].start()
        halos[-1].start()
    loads[2].wait()
    rows = mm(normed[...], wq[...]).astype(bf16)
    for g in range(GROUPS):
        qs[g] = rows[:, g * LANES : (g + 1) * LANES]

    def own_scores(g, carry):
        for sub in range(2):
            wts[2 * g + sub, 1] = mm_nt(qs[g] * mb[sub], kv[1, 0, g]) * scale + bias[1]
        return carry

    lax.fori_loop(0, GROUPS, own_scores, 0)
    for copy in halos:
        copy.wait_recv()

    def attend(g, carry):
        parts = []
        for sub in range(2):
            qm = qs[g] * mb[sub]
            score = [
                mm_nt(qm, kv[0, 0, g]) * scale + bias[0],
                wts[2 * g + sub, 1],
                mm_nt(qm, kv[2, 0, g]) * scale + bias[2],
            ]
            top = jnp.maximum(jnp.maximum(score[0], score[1]), score[2])
            top = jnp.max(top, axis=1, keepdims=True)
            lifted = [jnp.exp(x - top) for x in score]
            total = jnp.sum(lifted[0] + lifted[1] + lifted[2], axis=1, keepdims=True)
            inv = 1.0 / total
            acc = None
            for b in range(3):
                w = lifted[b] * inv
                wts[2 * g + sub, b] = w
                low = w.astype(bf16)
                wlow[2 * g + sub, b] = low
                term = mm(low, kv[b, 1, g])
                acc = term if acc is None else acc + term
            parts.append(acc * mf[sub])
        both = parts[0] + parts[1]
        att[g] = both
        columns = pl.ds(pl.multiple_of(g * LANES, LANES), LANES)
        res = (frame_ref[:, columns].astype(f32) + both).astype(bf16)
        res_low[g] = res
        res_ext[g, PAD : PAD + F, :] = res.astype(f32)
        return carry

    lax.fori_loop(0, GROUPS, attend, 0)

    def edges(low, halo, send, recv):
        return [
            remote(low.at[:, 0:PAD, :], halo.at[1], send.at[0], recv.at[0], {"seq": left}),
            remote(low.at[:, F - PAD : F, :], halo.at[0], send.at[1], recv.at[1], {"seq": right}),
        ]

    def place(halo, ext):
        for g in range(GROUPS):
            ext[g, 0:PAD, :] = halo[0, g].astype(f32)
            ext[g, PAD + F : 2 * PAD + F, :] = halo[1, g].astype(f32)

    res_edges = edges(res_low, res_halo, rh_send, rh_recv)
    for copy in res_edges:
        copy.start()

    def taps(ext, g, r, mirrored):
        base = seg_col[WIN + r : WIN + r + CHUNK, :]
        acc = jnp.zeros((CHUNK, LANES), f32)
        for t in range(KS):
            shift = (HALF_K - t) if mirrored else (t - HALF_K)
            same = seg_col[WIN + r + shift : WIN + r + shift + CHUNK, :] == base
            term = ext[g, PAD + r + shift : PAD + r + shift + CHUNK, :] * cw_ref[g, t : t + 1, :]
            acc = acc + jnp.where(same, term, 0.0)
        return acc

    def forward_conv(starts):
        def body(g, carry):
            columns = pl.ds(pl.multiple_of(g * LANES, LANES), LANES)
            for r in starts:
                conv = taps(res_ext, g, r, False)
                gate = lax.logistic(conv)
                out_ref[r : r + CHUNK, columns] = (
                    res_ext[g, PAD + r : PAD + r + CHUNK, :] + conv * gate
                ).astype(bf16)
                up = cot_ref[r : r + CHUNK, columns].astype(f32)
                gc = (up * gate * (1.0 + conv * (1.0 - gate))).astype(bf16)
                gc_low[g, r : r + CHUNK, :] = gc
                gc_ext[g, PAD + r : PAD + r + CHUNK, :] = gc.astype(f32)
            return carry

        lax.fori_loop(0, GROUPS, body, 0)

    def backward_conv(starts):
        def body(g, carry):
            columns = pl.ds(pl.multiple_of(g * LANES, LANES), LANES)
            for r in starts:
                moved = taps(gc_ext, g, r, True)
                up = cot_ref[r : r + CHUNK, columns].astype(f32)
                gres[g, r : r + CHUNK, :] = (up + moved).astype(bf16)
            return carry

        lax.fori_loop(0, GROUPS, body, 0)

    inner = (CHUNK, 2 * CHUNK)
    outer = (0, 3 * CHUNK)
    forward_conv(inner)
    for copy in res_edges:
        copy.wait_recv()
    place(res_halo, res_ext)
    forward_conv(outer)
    gc_edges = edges(gc_low, gc_halo, gh_send, gh_recv)
    for copy in gc_edges:
        copy.start()
    backward_conv(inner)
    for copy in gc_edges:
        copy.wait_recv()
    place(gc_halo, gc_ext)
    backward_conv(outer)

    def kv_grad_copies(g):
        return [
            remote(dsend.at[0, g], drecv.at[1, g], d_send.at[0, g], d_recv.at[1, g], {"seq": left}),
            remote(dsend.at[1, g], drecv.at[0, g], d_send.at[1, g], d_recv.at[0, g], {"seq": right}),
        ]

    def attend_back(g, carry):
        gq = []
        dk = [None, None, None]
        dv = [None, None, None]
        for sub in range(2):
            gm = gres[g] * mb[sub]
            qm = qs[g] * mb[sub]
            delta = jnp.sum(gm.astype(f32) * att[g], axis=1, keepdims=True)
            acc = None
            for b in range(3):
                gw = mm_nt(gm, kv[b, 1, g])
                ds = (wts[2 * g + sub, b] * (gw - delta) * scale).astype(bf16)
                term = mm(ds, kv[b, 0, g])
                acc = term if acc is None else acc + term
                dkt = mm_tn(ds, qm)
                dvt = mm_tn(wlow[2 * g + sub, b], gm)
                dk[b] = dkt if dk[b] is None else dk[b] + dkt
                dv[b] = dvt if dv[b] is None else dv[b] + dvt
            gq.append(acc * mf[sub])
        columns = pl.ds(pl.multiple_of(g * LANES, LANES), LANES)
        dq_ref[:, columns] = (gq[0] + gq[1]).astype(bf16)
        for slot, b in ((0, 0), (1, 2)):
            dsend[slot, g, 0] = dk[b].astype(bf16)
            dsend[slot, g, 1] = dv[b].astype(bf16)
        down[g, 0] = dk[1]
        down[g, 1] = dv[1]
        for copy in kv_grad_copies(g):
            copy.start()
        return carry

    lax.fori_loop(0, GROUPS, attend_back, 0)

    def weight_rows(ref, off):
        return ref[pl.ds(pl.multiple_of(peer(off) * PART, PART), PART), :]

    for off in (2, 1, 3, 0):
        pacc[off] = mm_nt(dq_ref[...], weight_rows(wq, off))

    for g in range(GROUPS):
        for copy in kv_grad_copies(g):
            copy.wait_recv()
        for which, dst in ((0, dkb), (1, dvb)):
            dst[:, g * LANES : (g + 1) * LANES] = (
                down[g, which] + drecv[0, g, which].astype(f32) + drecv[1, g, which].astype(f32)
            ).astype(bf16)

    row_sum = jnp.zeros((F, 1), f32)
    row_dot = jnp.zeros((F, 1), f32)
    exchanges = []
    for off in (2, 1, 3, 0):
        part = pacc[off] + mm_nt(dkb[...], weight_rows(wk, off)) + mm_nt(dvb[...], weight_rows(wv, off))
        part = part * gain_ref[peer(off)]
        row_sum = row_sum + jnp.sum(part, axis=1, keepdims=True)
        row_dot = row_dot + jnp.sum(part * unit[peer(off)], axis=1, keepdims=True)
        if off:
            psend[off - 1] = part.astype(bf16)
            copy = remote(
                psend.at[off - 1], precv.at[off - 1], p_send.at[off - 1], p_recv.at[off - 1], {"head": peer(off)}
            )
            copy.start()
            exchanges.append(copy)
        else:
            pacc[0] = part

    lanes = lax.broadcasted_iota(jnp.int32, (F, LANES), 1)
    packed = jnp.where(lanes == 0, row_sum, jnp.where(lanes == 1, row_dot, 0.0))
    ssend[...] = jnp.transpose(packed)[0:8, :]
    for off in (2, 1, 3):
        copy = remote(ssend, srecv.at[off - 1], s_send.at[off - 1], s_recv.at[off - 1], {"head": peer(off)})
        copy.start()
        exchanges.append(copy)
    for copy in exchanges:
        copy.wait_recv()
    sums = ssend[...] + srecv[0] + srecv[1] + srecv[2]
    sums = jnp.transpose(jnp.concatenate([sums] * (LANES // 8), axis=0)) * (1.0 / (HEADS_ALL * PART))
    inv_ref[:, 1:2] = sums[:, 0:1]
    inv_ref[:, 2:3] = sums[:, 1:2]

    def finish(r, carry):
        rows = pl.ds(pl.multiple_of(r * 32, 32), 32)
        scaled = pacc[0, rows, :]
        for i in range(3):
            scaled = scaled + precv[i, rows, :].astype(f32)
        through = inv_ref[rows, 0:1] * (
            scaled - inv_ref[rows, 1:2] - unit[me, rows, :] * inv_ref[rows, 2:3]
        )
        for g in range(GROUPS):
            columns = slice(g * LANES, (g + 1) * LANES)
            grad_ref[rows, columns] = (gres[g, rows, :].astype(f32) + through[:, columns]).astype(bf16)
        return carry

    lax.fori_loop(0, F // 32, finish, 0)

    for copy in gathers + halos + res_edges + gc_edges + exchanges:
        copy.wait_send()
    for g in range(GROUPS):
        for copy in kv_grad_copies(g):
            copy.wait_send()


def block_call(frame_part, segments, gain, wq, wk, wv, conv_weight, cotangent):
    f32, bf16 = jnp.float32, jnp.bfloat16
    span = F + 2 * WIN
    seg_row = segments[None, :]
    seg_col = jnp.broadcast_to(segments[:, None], (span, LANES))
    gain_parts = gain.reshape(HEADS_ALL, 1, PART)
    taps = jnp.pad(conv_weight, ((0, 1), (0, 0))).reshape(KS + 1, GROUPS, LANES)
    taps = jnp.transpose(taps, (1, 0, 2))
    vmem = pl.BlockSpec(memory_space=pltpu.VMEM)
    hbm = pl.BlockSpec(memory_space=pl.ANY)
    v = pltpu.VMEM
    dma = pltpu.SemaphoreType.DMA
    shape = jax.ShapeDtypeStruct((F, PART), bf16)
    return pl.pallas_call(
        block_kernel,
        out_shape=(shape, shape),
        in_specs=[vmem] * 6 + [hbm] * 3,
        out_specs=(vmem, vmem),
        scratch_shapes=[
            v((HEADS_ALL, F, PART), bf16),
            v((HEADS_ALL, F, PART), f32),
            v((F, HEADS_ALL * PART), bf16),
            v((F, LANES), f32),
            v((HEADS_ALL * PART, PART), bf16),
            v((HEADS_ALL * PART, PART), bf16),
            v((HEADS_ALL * PART, PART), bf16),
            v((3, 2, GROUPS, F, LANES), bf16),
            v((GROUPS, F, LANES), bf16),
            v((3, F, F), f32),
            v((2 * GROUPS, 3, F, F), f32),
            v((2 * GROUPS, 3, F, F), bf16),
            v((GROUPS, F, LANES), f32),
            v((GROUPS, F, LANES), bf16),
            v((GROUPS, F + 2 * PAD, LANES), f32),
            v((2, GROUPS, PAD, LANES), bf16),
            v((GROUPS, F, LANES), bf16),
            v((GROUPS, F + 2 * PAD, LANES), f32),
            v((2, GROUPS, PAD, LANES), bf16),
            v((GROUPS, F, LANES), bf16),
            v((F, PART), bf16),
            v((2, GROUPS, 2, F, LANES), bf16),
            v((2, GROUPS, 2, F, LANES), bf16),
            v((GROUPS, 2, F, LANES), f32),
            v((F, PART), bf16),
            v((F, PART), bf16),
            v((HEADS_ALL, F, PART), f32),
            v((3, F, PART), bf16),
            v((3, F, PART), bf16),
            v((8, F), f32),
            v((3, 8, F), f32),
            dma((3,)),
            dma((3,)),
            dma((3,)),
            dma((2, 2)),
            dma((2, 2)),
            dma((2,)),
            dma((2,)),
            dma((2,)),
            dma((2,)),
            dma((2, GROUPS)),
            dma((2, GROUPS)),
            dma((3,)),
            dma((3,)),
            dma((3,)),
            dma((3,)),
        ],
        compiler_params=pltpu.CompilerParams(
            collective_id=0, has_side_effects=True, vmem_limit_bytes=56 * 1024 * 1024
        ),
    )(frame_part, seg_row, seg_col, gain_parts, taps, cotangent, wq, wk, wv)


def on_device(loader_rows, plan, lengths, gain, wq, wk, wv, conv_weight, cotangent):
    seq_count = lax.axis_size("seq")
    seq_index = lax.axis_index("seq")
    frames, part_cols = cotangent.shape
    frame_total = frames * seq_count
    capacity = loader_rows.shape[0] // seq_count
    blocks = loader_rows.reshape(seq_count, capacity, part_cols)
    arrived = lax.all_to_all(blocks, "seq", split_axis=0, concat_axis=0, tiled=True)
    counts = lax.dynamic_slice_in_dim(plan, seq_index, 1, 1)[:, 0]
    running = jnp.cumsum(counts)
    slot_index = jnp.arange(frames, dtype=jnp.int32)
    source = jnp.sum((running[None, :] <= slot_index[:, None]).astype(jnp.int32), axis=1)
    earlier = jnp.arange(seq_count, dtype=jnp.int32)[None, :] < source[:, None]
    before = jnp.sum(jnp.where(earlier, counts[None, :], 0), axis=1)
    row_index = source * capacity + slot_index - before
    frame_part = jnp.take(arrived.reshape(seq_count * capacity, part_cols), row_index, axis=0)
    positions = seq_index * frames + jnp.arange(-WIN, frames + WIN, dtype=jnp.int32)
    segments = segment_ids(positions, lengths, frame_total)
    return block_call(frame_part, segments, gain, wq, wk, wv, conv_weight, cotangent)


def solution(mesh):
    placed = (
        P("seq", "head"),
        P(),
        P(),
        P(),
        P(None, "head"),
        P(None, "head"),
        P(None, "head"),
        P(None, "head"),
        P("seq", "head"),
    )
    return jax.shard_map(
        on_device,
        mesh=mesh,
        in_specs=placed,
        out_specs=(P("seq", "head"), P("seq", "head")),
        check_vma=False,
    )
```

time: 240 us -> 113 us (0.47)
  the two profiles are of different devices: /device:TPU:1 before, /device:TPU:32 now
where the time goes in v2:
time: 113 us
  Pallas kernels  57.6 us (51%)
  waiting for transfers between devices  24.3 us (22%)
  starting transfers between devices  19 us (17%)
  local copies, waits for them, and re-layouts  8.9 us (8%)
  other arithmetic  2.55 us (2%)
    pallas_call x1, Pallas kernels, block_call(): pl.pallas_call(block_kernel, out_shape=(shape, shape), in_specs=[vmem] *...  57.6 us
    all_to_all x1, waiting for transfers between devices, on_device(): lax.all_to_all(blocks, 'seq', split_axis=0, concat_axis=0, tiled=True)  24.3 us
    all_to_all x1, starting transfers between devices, on_device(): lax.all_to_all(blocks, 'seq', split_axis=0, concat_axis=0, tiled=True)  19 us
    unnamed x10, local copies, waits for them, and re-layouts  3.26 us
  transfers between devices with their start and end apart: 1, of which 1 were waited for; matrix products, arithmetic and copies ran while one was open for 3% of the time, Pallas kernels for 0%

profile of v2, /device:TPU:32, one launch (start us, length us, event | category | flops | bytes accessed | tf_op | source)
XLA Modules:
  0.0 113.2 jit_solution(1791565064942974249)
XLA Ops:
  0.6 0.0 copy-start
  0.6 0.0 copy-start.3
  0.7 0.0 copy-start.2
  0.7 0.0 copy-start.1
  0.7 1.9 %reshape.132 = bf16[128,4,384]{2,1,0:T(4,128)(2,1)} reshape(bf16[512,384]{1,0:T(8,128)(2,1)} %param.9) | data formatting | bytes 786432 | tf_op jit(solution)/shard_map/reshape | solution.py:442
  2.5 19.0 %all-to-all-start = ((bf16[128,4,384]{2,1,0:T(4,128)(2,1)}), bf16[128,4,384]{2,1,0:T(4,128)(2,1)S(1)}, u32[]{:S(2)}, u32[]{:S(2)}) async-start(bf16[128,4,384]{2,1,0:T(4,128)(2,1)} %reshape.132), calls=%async_computation | async-start | bytes 786432 | tf_op jit(solution)/shard_map/all_to_all | solution.py:443
  21.6 0.0 copy-done
  21.6 0.2 fusion
  21.7 0.2 reduce-window.19
  21.9 0.1 reduce
  22.0 0.0 copy-done.3
  22.1 0.3 reduce-window.20
  22.4 0.1 slice.10
  22.5 0.1 slice_reduce_fusion
  22.6 0.1 add_bitcast_fusion
  22.7 0.0 copy-done.2
  22.7 0.6 reshape.136.gain_ref
  23.3 0.1 convert_reduce_fusion
  23.4 0.6 and_select_fusion.seg_row
  24.0 0.1 convert_reduce_fusion.1
  24.1 0.2 select_reduce_fusion
  24.4 0.0 copy-done.1
  24.4 0.6 bitcast_bitcast_fusion.cw_ref
  25.0 24.3 %all-to-all-done = bf16[128,4,384]{2,1,0:T(4,128)(2,1)S(1)} async-done(((bf16[128,4,384]{2,1,0:T(4,128)(2,1)}), bf16[128,4,384]{2,1,0:T(4,128)(2,1)S(1)}, u32[]{:S(2)}, u32[]{:S(2)}) %all-to-all-start) | async-done | bytes 393248 | tf_op jit(solution)/shard_map/all_to_all | solution.py:443
  49.4 0.1 reshape.133
  49.5 1.2 %gather_fusion = bf16[256,384]{1,0:T(8,128)(2,1)S(1)} fusion(bf16[512,384]{1,0:T(8,128)(2,1)S(1)} %reshape.133, s32[1024]{0:T(1024)S(1)} %pad_clamp_fusion), kind=kCustom, calls=%fused_computation | custom fusion | bytes 394240 | tf_op jit(solution)/shard_map/jit(_take)/gather | solution.py:451
  50.6 0.8 broadcast_select_fusion.frame_ref
  51.4 0.9 broadcast_in_dim.50.seg_col
  52.3 57.6 %shard_map.104 = (bf16[256,384]{1,0:T(8,128)(2,1)}, bf16[256,384]{1,0:T(8,128)(2,1)}) custom-call(bf16[256,384]{1,0:T(8,128)(2,1)} %broadcast_select_fusion.frame_ref, s32[1,768]{1,0:T(1,128)} %and_select_fusion.seg_row, s32[768,128]{1,0:T(8,128)} %broadcast_in_dim.50.seg_col, f32[4,1,384]{2,1,0:T(1,128)} %reshape.136.gain_ref, ...), custom_call_target="tpu_custom_call" | custom-call | tf_op jit(solution)/shard_map/pallas_call | solution.py:377
  109.9 1.6 %copy.17 = bf16[256,384]{1,0:T(8,128)(2,1)} copy(bf16[256,384]{1,0:T(8,128)(2,1)} %get-tuple-element.6) | data formatting | bytes 393216
  111.6 1.6 %copy.18 = bf16[256,384]{1,0:T(8,128)(2,1)} copy(bf16[256,384]{1,0:T(8,128)(2,1)} %get-tuple-element.7) | data formatting | bytes 393216
  (8 shorter events, 0.1 us)
Async XLA Ops:
  0.6 20.9 %copy-start = (s32[128,128]{1,0:T(8,128)S(1)}, s32[128,128]{1,0:T(8,128)}, u32[]{:S(2)}) copy-start(s32[128,128]{1,0:T(8,128)} %param.10) | copy-start | bytes 196612
  0.6 21.4 %copy-start.3 = (s32[170]{0:T(256)S(1)}, s32[170]{0:T(256)}, u32[]{:S(2)}) copy-start(s32[170]{0:T(256)} %param.11) | copy-start | bytes 2044
  0.7 22.0 %copy-start.2 = (f32[1536]{0:T(1024)S(1)}, f32[1536]{0:T(1024)}, u32[]{:S(2)}) copy-start(f32[1536]{0:T(1024)} %param.12) | copy-start | bytes 18436
  0.7 23.7 %copy-start.1 = (f32[31,384]{1,0:T(8,128)S(1)}, f32[31,384]{1,0:T(8,128)}, u32[]{:S(2)}) copy-start(f32[31,384]{1,0:T(8,128)} %param.16) | copy-start | bytes 142852
  2.5 46.8 %all-to-all-start = ((bf16[128,4,384]{2,1,0:T(4,128)(2,1)}), bf16[128,4,384]{2,1,0:T(4,128)(2,1)S(1)}, u32[]{:S(2)}, u32[]{:S(2)}) async-start(bf16[128,4,384]{2,1,0:T(4,128)(2,1)} %reshape.132), calls=%async_computation | async-start | bytes 786432 | tf_op jit(solution)/shard_map/all_to_all | solution.py:443

commit v3 on v2

--- a/solution.py
+++ b/solution.py
@@ -24,13 +24,6 @@
 MESH = pl.DeviceIdType.MESH
 
 
-def segment_ids(positions, lengths, frame_total):
-    utter_ends = jnp.cumsum(lengths)
-    inside = (positions >= 0) & (positions < frame_total)
-    counted = jnp.sum((utter_ends[None, :] <= positions[:, None]).astype(jnp.int32), axis=1)
-    return jnp.where(inside, counted, -1)
-
-
 def mm(a, b):
     return jnp.dot(a, b, preferred_element_type=jnp.float32)
 
@@ -44,12 +37,12 @@
 
 
 def block_kernel(
-    frame_ref, seg_row, seg_col, gain_ref, cw_ref, cot_ref, wq_hbm, wk_hbm, wv_hbm,
+    plan_ref, len_ref, gain_all, cw_ref, cot_ref, loader, wq_hbm, wk_hbm, wv_hbm,
     out_ref, grad_ref,
-    gath, unit, normed, inv_ref, wq, wk, wv, kv, qs, bias, wts, wlow, att,
+    arr, par, hot, len_row, seg_row, seg_col, gain_ref, frame_ref, gath, unit, normed, inv_ref, wq, wk, wv, kv, qs, bias, wts, wlow, att,
     res_low, res_ext, res_halo, gc_low, gc_ext, gc_halo, gres,
     dq_ref, dsend, drecv, down, dkb, dvb, pacc, psend, precv, ssend, srecv,
-    w_sem, ag_send, ag_recv, kv_send, kv_recv, rh_send, rh_recv, gh_send, gh_recv,
+    a_send, a_recv, f_send, f_recv, own_sem, w_sem, ag_send, ag_recv, kv_send, kv_recv, rh_send, rh_recv, gh_send, gh_recv,
     d_send, d_recv, p_send, p_recv, s_send, s_recv,
 ):
     seq_count = lax.axis_size("seq")
@@ -75,12 +68,122 @@
     for copy in loads:
         copy.start()
 
+    pairs, tile = loader.shape[0], loader.shape[1]
+    slots, capacity = pairs * tile, tile // 2
+    half = pairs // 2
+    core = lax.rem(seq, 2)
+    pair = lax.div(seq, 2)
+    partner = seq + 1 - 2 * core
+    own_tile = pltpu.make_async_copy(loader.at[pair], arr.at[pair], own_sem.at[0])
+    own_tile.start()
+
     barrier = pltpu.get_barrier_semaphore()
+
+    def greet(j, carry):
+        pl.semaphore_signal(
+            barrier, inc=1, device_id={"seq": lax.rem(seq + 2 * j, seq_count)}, device_id_type=MESH
+        )
+        return carry
+
+    lax.fori_loop(1, pairs, greet, 0)
     for off in (1, 2, 3):
         pl.semaphore_signal(barrier, inc=1, device_id={"head": peer(off)}, device_id_type=MESH)
-    for side in (left, right):
+    for side in (left, right, partner):
         pl.semaphore_signal(barrier, inc=1, device_id={"seq": side}, device_id_type=MESH)
-    pl.semaphore_wait(barrier, 5)
+
+    for h in range(HEADS_ALL):
+        gain_ref[h] = gain_all[:, h * PART : (h + 1) * PART]
+    len_row[...] = jnp.zeros_like(len_row)
+    len_row[0:1, 0 : len_ref.shape[1]] = len_ref[...].astype(f32)
+    rows_i = lax.broadcasted_iota(jnp.int32, (F, F), 0)
+    cols_i = lax.broadcasted_iota(jnp.int32, (F, F), 1)
+    pl.semaphore_wait(barrier, pairs + 5)
+
+    def slot_copy(j):
+        there = lax.rem(pair + j, pairs)
+        return remote(
+            loader.at[there], arr.at[pair], a_send.at[j], a_recv.at[j], {"seq": lax.rem(seq + 2 * j, seq_count)}
+        )
+
+    def pass_on(j):
+        slot = lax.rem(pair + pairs - j, pairs)
+        return remote(arr.at[slot], par.at[slot], f_send.at[j], f_recv.at[j], {"seq": partner})
+
+    own_pass = remote(loader.at[pair], par.at[pair], f_send.at[0], f_recv.at[0], {"seq": partner})
+
+    def both_ways(act):
+        act(half)
+
+        def body(i, carry):
+            act(half - i)
+            act(half + i)
+            return carry
+
+        lax.fori_loop(1, half, body, 0)
+
+    both_ways(lambda j: slot_copy(j).start())
+    own_pass.start()
+
+    lens = len_row[0:1, :]
+    ends_col = jnp.sum(jnp.where(cols_i <= rows_i, lens, 0.0), axis=1, keepdims=True)
+    lens_col = jnp.transpose(jnp.broadcast_to(lens, (LANES, F)))[:, 0:1]
+    ends_row = jnp.sum(jnp.where(rows_i <= cols_i, lens_col, 0.0), axis=0, keepdims=True)
+    total = (seq_count * F) * 1.0
+    first = (seq * F - WIN).astype(f32)
+    for b in range(3):
+        place_row = lax.broadcasted_iota(jnp.int32, (1, F), 1).astype(f32) + (first + b * F)
+        inside = (place_row >= 0.0) & (place_row < total)
+        count = jnp.sum((ends_col <= place_row).astype(f32), axis=0, keepdims=True)
+        seg_row[0:1, b * F : (b + 1) * F] = jnp.where(inside, count, -1.0)
+        place_col = lax.broadcasted_iota(jnp.int32, (F, 1), 0).astype(f32) + (first + b * F)
+        inside = (place_col >= 0.0) & (place_col < total)
+        count = jnp.sum((ends_row <= place_col).astype(f32), axis=1, keepdims=True)
+        seg_col[b * F : (b + 1) * F, :] = jnp.broadcast_to(jnp.where(inside, count, -1.0), (F, LANES))
+
+    own_seg = seg_col[WIN : WIN + F, 0:1]
+    for b in range(3):
+        ok = seg_row[0:1, b * F : (b + 1) * F] == own_seg
+        if b == 0:
+            ok = ok & (cols_i >= rows_i)
+        if b == 2:
+            ok = ok & (cols_i < rows_i)
+        bias[b] = jnp.where(ok, 0.0, -jnp.inf)
+
+    lane = lax.broadcasted_iota(jnp.int32, (1, LANES), 1)
+    mf = [(lane < HEAD_DIM).astype(f32), (lane >= HEAD_DIM).astype(f32)]
+    mb = [m.astype(bf16) for m in mf]
+
+    chosen = (lax.broadcasted_iota(jnp.int32, (8, seq_count), 1) == seq).astype(f32).astype(bf16)
+    counts = mm_nt(chosen, plan_ref[...].astype(f32).astype(bf16)).astype(bf16)
+    lower = lax.broadcasted_iota(jnp.int32, (seq_count, seq_count), 0)
+    upper = lax.broadcasted_iota(jnp.int32, (seq_count, seq_count), 1)
+    starts = mm(counts, (lower < upper).astype(f32).astype(bf16)).astype(bf16)
+    loader_row = lax.broadcasted_iota(jnp.int32, (seq_count, slots), 0)
+    slot_pair = lax.shift_right_logical(
+        lax.broadcasted_iota(jnp.int32, (seq_count, slots), 1), jnp.int32(tile.bit_length() - 1)
+    )
+    slot_row = lax.broadcasted_iota(jnp.int32, (1, slots), 1)
+    slot_core = lax.shift_right_logical(slot_row, jnp.int32(capacity.bit_length() - 1)) & 1
+    within = (slot_row & (capacity - 1)).astype(f32)
+    frame_rows = lax.broadcasted_iota(jnp.int32, (F, slots), 0).astype(f32)
+    for which, parity in ((0, core), (1, 1 - core)):
+        spread = (loader_row == 2 * slot_pair + parity).astype(f32).astype(bf16)
+        count = mm(counts, spread)[0:1, :]
+        start = mm(starts, spread)[0:1, :]
+        target = jnp.where((slot_core == core) & (within < count), start + within, -1.0)
+        hot[which] = (frame_rows == target).astype(f32).astype(bf16)
+
+    def land(j):
+        slot_copy(j).wait_recv()
+        pass_on(j).start()
+
+    both_ways(land)
+    own_tile.wait()
+    own_pass.wait_recv()
+    both_ways(lambda j: pass_on(j).wait_recv())
+    frame_ref[...] = (
+        mm(hot[0], arr[...].reshape(slots, PART)) + mm(hot[1], par[...].reshape(slots, PART))
+    ).astype(bf16)
 
     gathers = [
         remote(frame_ref, gath.at[me], ag_send.at[off - 1], ag_recv.at[off - 1], {"head": peer(off)})
@@ -89,21 +192,6 @@
     for copy in gathers:
         copy.start()
     gath[me] = frame_ref[...]
-
-    rows_i = lax.broadcasted_iota(jnp.int32, (F, F), 0)
-    cols_i = lax.broadcasted_iota(jnp.int32, (F, F), 1)
-    own_seg = seg_col[WIN : WIN + F, 0:1]
-    for b in range(3):
-        ok = seg_row[:, b * F : (b + 1) * F] == own_seg
-        if b == 0:
-            ok = ok & (cols_i >= rows_i)
-        if b == 2:
-            ok = ok & (cols_i < rows_i)
-        bias[b] = jnp.where(ok, 0.0, -jnp.inf)
-
-    lane = lax.broadcasted_iota(jnp.int32, (1, LANES), 1)
-    mf = [(lane < HEAD_DIM).astype(f32), (lane >= HEAD_DIM).astype(f32)]
-    mb = [m.astype(bf16) for m in mf]
 
     for copy in gathers:
         copy.wait_recv()
@@ -207,7 +295,7 @@
         for t in range(KS):
             shift = (HALF_K - t) if mirrored else (t - HALF_K)
             same = seg_col[WIN + r + shift : WIN + r + shift + CHUNK, :] == base
-            term = ext[g, PAD + r + shift : PAD + r + shift + CHUNK, :] * cw_ref[g, t : t + 1, :]
+            term = ext[g, PAD + r + shift : PAD + r + shift + CHUNK, :] * cw_ref[t : t + 1, pl.ds(pl.multiple_of(g * LANES, LANES), LANES)]
             acc = acc + jnp.where(same, term, 0.0)
         return acc
 
@@ -354,6 +442,9 @@
 
     lax.fori_loop(0, F // 32, finish, 0)
 
+    both_ways(lambda j: slot_copy(j).wait_send())
+    both_ways(lambda j: pass_on(j).wait_send())
+    own_pass.wait_send()
     for copy in gathers + halos + res_edges + gc_edges + exchanges:
         copy.wait_send()
     for g in range(GROUPS):
@@ -361,14 +452,14 @@
             copy.wait_send()
 
 
-def block_call(frame_part, segments, gain, wq, wk, wv, conv_weight, cotangent):
+def block_call(loader_rows, plan, lengths, gain, wq, wk, wv, conv_weight, cotangent):
     f32, bf16 = jnp.float32, jnp.bfloat16
+    seq_count = lax.axis_size("seq")
     span = F + 2 * WIN
-    seg_row = segments[None, :]
-    seg_col = jnp.broadcast_to(segments[:, None], (span, LANES))
-    gain_parts = gain.reshape(HEADS_ALL, 1, PART)
-    taps = jnp.pad(conv_weight, ((0, 1), (0, 0))).reshape(KS + 1, GROUPS, LANES)
-    taps = jnp.transpose(taps, (1, 0, 2))
+    pairs = seq_count // 2
+    tile = loader_rows.shape[0] // pairs
+    slots = pairs * tile
+    loader = loader_rows.reshape(pairs, tile, PART)
     vmem = pl.BlockSpec(memory_space=pltpu.VMEM)
     hbm = pl.BlockSpec(memory_space=pl.ANY)
     v = pltpu.VMEM
@@ -377,9 +468,17 @@
     return pl.pallas_call(
         block_kernel,
         out_shape=(shape, shape),
-        in_specs=[vmem] * 6 + [hbm] * 3,
+        in_specs=[vmem] * 5 + [hbm] * 4,
         out_specs=(vmem, vmem),
         scratch_shapes=[
+            v((pairs, tile, PART), bf16),
+            v((pairs, tile, PART), bf16),
+            v((2, F, slots), bf16),
+            v((8, F), f32),
+            v((8, span), f32),
+            v((span, LANES), f32),
+            v((HEADS_ALL, 1, PART), f32),
+            v((F, PART), bf16),
             v((HEADS_ALL, F, PART), bf16),
             v((HEADS_ALL, F, PART), f32),
             v((F, HEADS_ALL * PART), bf16),
@@ -411,6 +510,11 @@
             v((3, F, PART), bf16),
             v((8, F), f32),
             v((3, 8, F), f32),
+            dma((pairs,)),
+            dma((pairs,)),
+            dma((pairs,)),
+            dma((pairs,)),
+            dma((1,)),
             dma((3,)),
             dma((3,)),
             dma((3,)),
@@ -430,28 +534,11 @@
         compiler_params=pltpu.CompilerParams(
             collective_id=0, has_side_effects=True, vmem_limit_bytes=56 * 1024 * 1024
         ),
-    )(frame_part, seg_row, seg_col, gain_parts, taps, cotangent, wq, wk, wv)
+    )(plan, lengths[None, :], gain[None, :], conv_weight, cotangent, loader, wq, wk, wv)
 
 
 def on_device(loader_rows, plan, lengths, gain, wq, wk, wv, conv_weight, cotangent):
-    seq_count = lax.axis_size("seq")
-    seq_index = lax.axis_index("seq")
-    frames, part_cols = cotangent.shape
-    frame_total = frames * seq_count
-    capacity = loader_rows.shape[0] // seq_count
-    blocks = loader_rows.reshape(seq_count, capacity, part_cols)
-    arrived = lax.all_to_all(blocks, "seq", split_axis=0, concat_axis=0, tiled=True)
-    counts = lax.dynamic_slice_in_dim(plan, seq_index, 1, 1)[:, 0]
-    running = jnp.cumsum(counts)
-    slot_index = jnp.arange(frames, dtype=jnp.int32)
-    source = jnp.sum((running[None, :] <= slot_index[:, None]).astype(jnp.int32), axis=1)
-    earlier = jnp.arange(seq_count, dtype=jnp.int32)[None, :] < source[:, None]
-    before = jnp.sum(jnp.where(earlier, counts[None, :], 0), axis=1)
-    row_index = source * capacity + slot_index - before
-    frame_part = jnp.take(arrived.reshape(seq_count * capacity, part_cols), row_index, axis=0)
-    positions = seq_index * frames + jnp.arange(-WIN, frames + WIN, dtype=jnp.int32)
-    segments = segment_ids(positions, lengths, frame_total)
-    return block_call(frame_part, segments, gain, wq, wk, wv, conv_weight, cotangent)
+    return block_call(loader_rows, plan, lengths, gain, wq, wk, wv, conv_weight, cotangent)
 
 
 def solution(mesh):

time: 113 us -> 104 us (0.920)
  the two profiles are of different devices: /device:TPU:32 before, /device:TPU:1 now
where the time goes in v3:
time: 104 us; the launch traced here: 103 us
  Pallas kernels  98.1 us (94%)
  local copies, waits for them, and re-layouts  4.54 us (4%)
    pallas_call x1, Pallas kernels, block_call(): pl.pallas_call(block_kernel, out_shape=(shape, shape), in_specs=[vmem] *...  98.1 us
    unnamed x2, local copies, waits for them, and re-layouts  3.25 us

profile of v3, /device:TPU:1, one launch (start us, length us, event | category | flops | bytes accessed | tf_op | source)
XLA Modules:
  0.0 103.3 jit_solution(5106002892195335632)
XLA Ops:
  0.6 1.3 %broadcast_in_dim.7.gain_all = f32[1,1536]{1,0:T(1,128)} reshape(f32[1536]{0:T(1024)} %param.12) | data formatting | bytes 12288 | tf_op jit(solution)/shard_map/broadcast_in_dim | solution.py:537
  1.9 98.1 %shard_map.104 = (bf16[256,384]{1,0:T(8,128)(2,1)}, bf16[256,384]{1,0:T(8,128)(2,1)}) custom-call(s32[128,128]{1,0:T(8,128)} %plan_ref.1, s32[1,170]{1,0:T(1,128)} %bitcast.3, f32[1,1536]{1,0:T(1,128)} %broadcast_in_dim.7.gain_all, f32[31,384]{1,0:T(8,128)} %cw_ref.1, bf16[256,384]{1,0:T(8,128)(2,1)} %cot_ref.1, bf16[64,8,384]{2,1,0:T(8,128)(2,1)} %bitcast.2, ...), custom_call_target="tpu_custom_call" | custom-call | tf_op jit(solution)/shard_map/pallas_call | solution.py:468
  100.0 1.6 %copy.13 = bf16[256,384]{1,0:T(8,128)(2,1)} copy(bf16[256,384]{1,0:T(8,128)(2,1)} %get-tuple-element.4) | data formatting | bytes 393216
  101.6 1.6 %copy.14 = bf16[256,384]{1,0:T(8,128)(2,1)} copy(bf16[256,384]{1,0:T(8,128)(2,1)} %get-tuple-element.5) | data formatting | bytes 393216

commit v4 on v3

--- a/solution.py
+++ b/solution.py
@@ -39,10 +39,10 @@
 def block_kernel(
     plan_ref, len_ref, gain_all, cw_ref, cot_ref, loader, wq_hbm, wk_hbm, wv_hbm,
     out_ref, grad_ref,
-    arr, par, hot, len_row, seg_row, seg_col, gain_ref, frame_ref, gath, unit, normed, inv_ref, wq, wk, wv, kv, qs, bias, wts, wlow, att,
+    zin, arr, par, hot, len_row, seg_row, seg_col, gain_ref, frame_ref, gath, unit, normed, inv_ref, wq, wk, wv, kv, qs, bias, wts, wlow, att,
     res_low, res_ext, res_halo, gc_low, gc_ext, gc_halo, gres,
-    dq_ref, dsend, drecv, down, dkb, dvb, pacc, psend, precv, ssend, srecv,
-    a_send, a_recv, f_send, f_recv, own_sem, w_sem, ag_send, ag_recv, kv_send, kv_recv, rh_send, rh_recv, gh_send, gh_recv,
+    dq_ref, dsend, drecv, down, dkb, dvb, pacc, psend, relay, precv, ssend, srecv,
+    z_send, z_recv, x_send, x_recv, l_sem, f_send, f_recv, own_sem, w_sem, ag_send, ag_recv, kv_send, kv_recv, rh_send, rh_recv, gh_send, gh_recv,
     d_send, d_recv, p_send, p_recv, s_send, s_recv,
 ):
     seq_count = lax.axis_size("seq")
@@ -68,24 +68,27 @@
     for copy in loads:
         copy.start()
 
-    pairs, tile = loader.shape[0], loader.shape[1]
-    slots, capacity = pairs * tile, tile // 2
-    half = pairs // 2
+    deep, wide, tile = loader.shape[0], loader.shape[1], loader.shape[2]
+    slots, capacity = deep * wide * tile, tile // 2
     core = lax.rem(seq, 2)
     pair = lax.div(seq, 2)
+    z, x = lax.div(pair, wide), lax.rem(pair, wide)
     partner = seq + 1 - 2 * core
-    own_tile = pltpu.make_async_copy(loader.at[pair], arr.at[pair], own_sem.at[0])
+    own_tile = pltpu.make_async_copy(loader.at[z], zin.at[z], own_sem.at[0])
     own_tile.start()
+    order = sorted(range(1, deep), key=lambda j: -min(j, deep - j))
+
+    def at_z(j):
+        return (lax.rem(z + j, deep) * wide + x) * 2 + core
+
+    def at_x(k):
+        return (z * wide + lax.rem(x + k, wide)) * 2 + core
 
     barrier = pltpu.get_barrier_semaphore()
-
-    def greet(j, carry):
-        pl.semaphore_signal(
-            barrier, inc=1, device_id={"seq": lax.rem(seq + 2 * j, seq_count)}, device_id_type=MESH
-        )
-        return carry
-
-    lax.fori_loop(1, pairs, greet, 0)
+    for j in order:
+        pl.semaphore_signal(barrier, inc=1, device_id={"seq": at_z(j)}, device_id_type=MESH)
+    for k in range(1, wide):
+        pl.semaphore_signal(barrier, inc=1, device_id={"seq": at_x(k)}, device_id_type=MESH)
     for off in (1, 2, 3):
         pl.semaphore_signal(barrier, inc=1, device_id={"head": peer(off)}, device_id_type=MESH)
     for side in (left, right, partner):
@@ -97,32 +100,37 @@
     len_row[0:1, 0 : len_ref.shape[1]] = len_ref[...].astype(f32)
     rows_i = lax.broadcasted_iota(jnp.int32, (F, F), 0)
     cols_i = lax.broadcasted_iota(jnp.int32, (F, F), 1)
-    pl.semaphore_wait(barrier, pairs + 5)
-
-    def slot_copy(j):
-        there = lax.rem(pair + j, pairs)
+    pl.semaphore_wait(barrier, deep + wide + 4)
+
+    def far(j):
         return remote(
-            loader.at[there], arr.at[pair], a_send.at[j], a_recv.at[j], {"seq": lax.rem(seq + 2 * j, seq_count)}
+            loader.at[lax.rem(z + j, deep)], zin.at[z], z_send.at[j], z_recv.at[j], {"seq": at_z(j)}
         )
 
+    def spread_out(j):
+        layer = lax.rem(z + deep - j, deep)
+        return [
+            remote(
+                zin.at[layer, lax.rem(x + k, wide)], arr.at[layer, x],
+                x_send.at[j, k], x_recv.at[j, k], {"seq": at_x(k)},
+            )
+            for k in range(1, wide)
+        ]
+
+    def keep(j):
+        layer = lax.rem(z + deep - j, deep)
+        return pltpu.make_async_copy(zin.at[layer, x], arr.at[layer, x], l_sem.at[j])
+
     def pass_on(j):
-        slot = lax.rem(pair + pairs - j, pairs)
-        return remote(arr.at[slot], par.at[slot], f_send.at[j], f_recv.at[j], {"seq": partner})
-
-    own_pass = remote(loader.at[pair], par.at[pair], f_send.at[0], f_recv.at[0], {"seq": partner})
-
-    def both_ways(act):
-        act(half)
-
-        def body(i, carry):
-            act(half - i)
-            act(half + i)
-            return carry
-
-        lax.fori_loop(1, half, body, 0)
-
-    both_ways(lambda j: slot_copy(j).start())
-    own_pass.start()
+        layer = lax.rem(z + deep - j, deep)
+        return remote(arr.at[layer], par.at[layer], f_send.at[j], f_recv.at[j], {"seq": partner})
+
+    for j in order:
+        far(j).start()
+    own_tile.wait()
+    keep(0).start()
+    for copy in spread_out(0):
+        copy.start()
 
     lens = len_row[0:1, :]
     ends_col = jnp.sum(jnp.where(cols_i <= rows_i, lens, 0.0), axis=1, keepdims=True)
@@ -173,28 +181,52 @@
         target = jnp.where((slot_core == core) & (within < count), start + within, -1.0)
         hot[which] = (frame_rows == target).astype(f32).astype(bf16)
 
-    def land(j):
-        slot_copy(j).wait_recv()
+    def settle(j):
+        for copy in spread_out(j):
+            copy.wait_recv()
+        keep(j).wait()
         pass_on(j).start()
 
-    both_ways(land)
-    own_tile.wait()
-    own_pass.wait_recv()
-    both_ways(lambda j: pass_on(j).wait_recv())
+    waiting = [0]
+    for j in order:
+        far(j).wait_recv()
+        keep(j).start()
+        for copy in spread_out(j):
+            copy.start()
+        waiting.append(j)
+        if len(waiting) > 3:
+            settle(waiting.pop(0))
+    for j in waiting:
+        settle(j)
+    for j in [0] + order:
+        pass_on(j).wait_recv()
     frame_ref[...] = (
         mm(hot[0], arr[...].reshape(slots, PART)) + mm(hot[1], par[...].reshape(slots, PART))
     ).astype(bf16)
 
+    low, high = pl.ds(0, F // 2), pl.ds(F // 2, F // 2)
+    up, down_by = {"head": peer(1)}, {"head": peer(3)}
+
+    def gather_copy(i, src, slot, rows, where):
+        return remote(src, gath.at[slot, rows, :], ag_send.at[i], ag_recv.at[i], where)
+
     gathers = [
-        remote(frame_ref, gath.at[me], ag_send.at[off - 1], ag_recv.at[off - 1], {"head": peer(off)})
-        for off in (2, 1, 3)
+        gather_copy(0, frame_ref.at[low, :], me, low, up),
+        gather_copy(1, frame_ref.at[high, :], me, high, up),
+        gather_copy(2, frame_ref.at[high, :], me, high, down_by),
+        gather_copy(3, frame_ref.at[low, :], me, low, down_by),
+        gather_copy(4, gath.at[peer(3), low, :], peer(3), low, up),
+        gather_copy(5, gath.at[peer(1), high, :], peer(1), high, down_by),
     ]
-    for copy in gathers:
-        copy.start()
+    for i in (0, 2, 1, 3):
+        gathers[i].start()
     gath[me] = frame_ref[...]
-
-    for copy in gathers:
-        copy.wait_recv()
+    gathers[0].wait_recv()
+    gathers[4].start()
+    gathers[2].wait_recv()
+    gathers[5].start()
+    for i in (1, 3, 4, 5):
+        gathers[i].wait_recv()
 
     def norm_rows(r, carry):
         rows = pl.ds(pl.multiple_of(r * 32, 32), 32)
@@ -397,30 +429,53 @@
 
     row_sum = jnp.zeros((F, 1), f32)
     row_dot = jnp.zeros((F, 1), f32)
-    exchanges = []
+    exchanges = [
+        remote(src.at[rows, :], dst.at[rows, :], p_send.at[i], p_recv.at[i], where)
+        for i, (src, dst, rows, where) in enumerate((
+            (psend.at[0], relay, low, up),
+            (psend.at[0], relay, high, down_by),
+            (psend.at[1], precv.at[0], high, up),
+            (psend.at[2], precv.at[1], low, down_by),
+            (psend.at[1], precv.at[0], low, up),
+            (psend.at[2], precv.at[1], high, down_by),
+        ))
+    ]
     for off in (2, 1, 3, 0):
         part = pacc[off] + mm_nt(dkb[...], weight_rows(wk, off)) + mm_nt(dvb[...], weight_rows(wv, off))
         part = part * gain_ref[peer(off)]
         row_sum = row_sum + jnp.sum(part, axis=1, keepdims=True)
         row_dot = row_dot + jnp.sum(part * unit[peer(off)], axis=1, keepdims=True)
-        if off:
-            psend[off - 1] = part.astype(bf16)
-            copy = remote(
-                psend.at[off - 1], precv.at[off - 1], p_send.at[off - 1], p_recv.at[off - 1], {"head": peer(off)}
-            )
-            copy.start()
-            exchanges.append(copy)
+        if off == 2:
+            psend[0] = part.astype(bf16)
+            exchanges[0].start()
+            exchanges[1].start()
+        elif off == 1:
+            pacc[1] = part
+            psend[1, high, :] = part[F // 2 :, :].astype(bf16)
+            exchanges[2].start()
+        elif off == 3:
+            pacc[3] = part
+            psend[2, low, :] = part[: F // 2, :].astype(bf16)
+            exchanges[3].start()
         else:
             pacc[0] = part
 
     lanes = lax.broadcasted_iota(jnp.int32, (F, LANES), 1)
     packed = jnp.where(lanes == 0, row_sum, jnp.where(lanes == 1, row_dot, 0.0))
     ssend[...] = jnp.transpose(packed)[0:8, :]
-    for off in (2, 1, 3):
-        copy = remote(ssend, srecv.at[off - 1], s_send.at[off - 1], s_recv.at[off - 1], {"head": peer(off)})
+    exchanges[0].wait_recv()
+    psend[1, low, :] = (pacc[1, low, :] + relay[low, :].astype(f32)).astype(bf16)
+    exchanges[4].start()
+    exchanges[1].wait_recv()
+    psend[2, high, :] = (pacc[3, high, :] + relay[high, :].astype(f32)).astype(bf16)
+    exchanges[5].start()
+    shared = [
+        remote(ssend, srecv.at[off - 1], s_send.at[off - 1], s_recv.at[off - 1], {"head": peer(off)})
+        for off in (2, 1, 3)
+    ]
+    for copy in shared:
         copy.start()
-        exchanges.append(copy)
-    for copy in exchanges:
+    for copy in exchanges[2:] + shared:
         copy.wait_recv()
     sums = ssend[...] + srecv[0] + srecv[1] + srecv[2]
     sums = jnp.transpose(jnp.concatenate([sums] * (LANES // 8), axis=0)) * (1.0 / (HEADS_ALL * PART))
@@ -430,7 +485,7 @@
     def finish(r, carry):
         rows = pl.ds(pl.multiple_of(r * 32, 32), 32)
         scaled = pacc[0, rows, :]
-        for i in range(3):
+        for i in range(2):
             scaled = scaled + precv[i, rows, :].astype(f32)
         through = inv_ref[rows, 0:1] * (
             scaled - inv_ref[rows, 1:2] - unit[me, rows, :] * inv_ref[rows, 2:3]
@@ -442,10 +497,13 @@
 
     lax.fori_loop(0, F // 32, finish, 0)
 
-    both_ways(lambda j: slot_copy(j).wait_send())
-    both_ways(lambda j: pass_on(j).wait_send())
-    own_pass.wait_send()
-    for copy in gathers + halos + res_edges + gc_edges + exchanges:
+    for j in [0] + order:
+        if j:
+            far(j).wait_send()
+        pass_on(j).wait_send()
+        for copy in spread_out(j):
+            copy.wait_send()
+    for copy in gathers + halos + res_edges + gc_edges + exchanges + shared:
         copy.wait_send()
     for g in range(GROUPS):
         for copy in kv_grad_copies(g):
@@ -459,7 +517,9 @@
     pairs = seq_count // 2
     tile = loader_rows.shape[0] // pairs
     slots = pairs * tile
-    loader = loader_rows.reshape(pairs, tile, PART)
+    wide = 4 if pairs > 8 else 2
+    deep = pairs // wide
+    loader = loader_rows.reshape(deep, wide, tile, PART)
     vmem = pl.BlockSpec(memory_space=pltpu.VMEM)
     hbm = pl.BlockSpec(memory_space=pl.ANY)
     v = pltpu.VMEM
@@ -471,8 +531,9 @@
         in_specs=[vmem] * 5 + [hbm] * 4,
         out_specs=(vmem, vmem),
         scratch_shapes=[
-            v((pairs, tile, PART), bf16),
-            v((pairs, tile, PART), bf16),
+            v((deep, wide, tile, PART), bf16),
+            v((deep, wide, tile, PART), bf16),
+            v((deep, wide, tile, PART), bf16),
             v((2, F, slots), bf16),
             v((8, F), f32),
             v((8, span), f32),
@@ -507,17 +568,21 @@
             v((F, PART), bf16),
             v((HEADS_ALL, F, PART), f32),
             v((3, F, PART), bf16),
-            v((3, F, PART), bf16),
+            v((F, PART), bf16),
+            v((2, F, PART), bf16),
             v((8, F), f32),
             v((3, 8, F), f32),
-            dma((pairs,)),
-            dma((pairs,)),
-            dma((pairs,)),
-            dma((pairs,)),
+            dma((deep,)),
+            dma((deep,)),
+            dma((deep, wide)),
+            dma((deep, wide)),
+            dma((deep,)),
+            dma((deep,)),
+            dma((deep,)),
             dma((1,)),
             dma((3,)),
-            dma((3,)),
-            dma((3,)),
+            dma((6,)),
+            dma((6,)),
             dma((2, 2)),
             dma((2, 2)),
             dma((2,)),
@@ -526,8 +591,8 @@
             dma((2,)),
             dma((2, GROUPS)),
             dma((2, GROUPS)),
-            dma((3,)),
-            dma((3,)),
+            dma((6,)),
+            dma((6,)),
             dma((3,)),
             dma((3,)),
         ],

time: 104 us -> 106 us (1.019)
  the two profiles are of different devices: /device:TPU:1 before, /device:TPU:8 now
where the time goes in v4:
time: 106 us
  Pallas kernels  101 us (95%)
  local copies, waits for them, and re-layouts  4.54 us (4%)
    pallas_call x1, Pallas kernels, block_call(): pl.pallas_call(block_kernel, out_shape=(shape, shape), in_specs=[vmem] *...  101 us
    unnamed x2, local copies, waits for them, and re-layouts  3.25 us

profile of v4, /device:TPU:8, one launch (start us, length us, event | category | flops | bytes accessed | tf_op | source)
XLA Modules:
  0.0 106.3 jit_solution(8975712397866998436)
XLA Ops:
  0.6 1.3 %broadcast_in_dim.7.gain_all = f32[1,1536]{1,0:T(1,128)} reshape(f32[1536]{0:T(1024)} %param.12) | data formatting | bytes 12288 | tf_op jit(solution)/shard_map/broadcast_in_dim | solution.py:602
  1.9 101.1 %shard_map.104 = (bf16[256,384]{1,0:T(8,128)(2,1)}, bf16[256,384]{1,0:T(8,128)(2,1)}) custom-call(s32[128,128]{1,0:T(8,128)} %plan_ref.1, s32[1,170]{1,0:T(1,128)} %bitcast.3, f32[1,1536]{1,0:T(1,128)} %broadcast_in_dim.7.gain_all, f32[31,384]{1,0:T(8,128)} %cw_ref.1, bf16[256,384]{1,0:T(8,128)(2,1)} %cot_ref.1, bf16[16,4,8,384]{3,2,1,0:T(8,128)(2,1)} %bitcast.2, ...), custom_call_target="tpu_custom_call" | custom-call | tf_op jit(solution)/shard_map/pallas_call | solution.py:528
  103.0 1.6 %copy.13 = bf16[256,384]{1,0:T(8,128)(2,1)} copy(bf16[256,384]{1,0:T(8,128)(2,1)} %get-tuple-element.4) | data formatting | bytes 393216
  104.6 1.6 %copy.14 = bf16[256,384]{1,0:T(8,128)(2,1)} copy(bf16[256,384]{1,0:T(8,128)(2,1)} %get-tuple-element.5) | data formatting | bytes 393216

commit v5 on v3

--- a/solution.py
+++ b/solution.py
@@ -39,10 +39,10 @@
 def block_kernel(
     plan_ref, len_ref, gain_all, cw_ref, cot_ref, loader, wq_hbm, wk_hbm, wv_hbm,
     out_ref, grad_ref,
-    arr, par, hot, len_row, seg_row, seg_col, gain_ref, frame_ref, gath, unit, normed, inv_ref, wq, wk, wv, kv, qs, bias, wts, wlow, att,
+    xin, arr, par, hot, len_row, seg_row, seg_col, gain_ref, frame_ref, gath, unit, normed, inv_ref, wq, wk, wv, kv, qs, bias, wts, wlow, att,
     res_low, res_ext, res_halo, gc_low, gc_ext, gc_halo, gres,
     dq_ref, dsend, drecv, down, dkb, dvb, pacc, psend, precv, ssend, srecv,
-    a_send, a_recv, f_send, f_recv, own_sem, w_sem, ag_send, ag_recv, kv_send, kv_recv, rh_send, rh_recv, gh_send, gh_recv,
+    z_send, z_recv, x_send, x_recv, l_sem, f_send, f_recv, w_sem, ag_send, ag_recv, kv_send, kv_recv, rh_send, rh_recv, gh_send, gh_recv,
     d_send, d_recv, p_send, p_recv, s_send, s_recv,
 ):
     seq_count = lax.axis_size("seq")
@@ -68,61 +68,84 @@
     for copy in loads:
         copy.start()
 
-    pairs, tile = loader.shape[0], loader.shape[1]
-    slots, capacity = pairs * tile, tile // 2
-    half = pairs // 2
+    deep, wide, tile = loader.shape[0], loader.shape[1], loader.shape[2]
+    slots, capacity = deep * wide * tile, tile // 2
     core = lax.rem(seq, 2)
     pair = lax.div(seq, 2)
+    z, x = lax.div(pair, wide), lax.rem(pair, wide)
     partner = seq + 1 - 2 * core
-    own_tile = pltpu.make_async_copy(loader.at[pair], arr.at[pair], own_sem.at[0])
-    own_tile.start()
+    half = deep // 2
+    steps = sorted(range(1, wide), key=lambda k: min(k, wide - k))
+
+    def at_z(j):
+        return (lax.rem(z + j, deep) * wide + x) * 2 + core
+
+    def at_x(k):
+        return (z * wide + lax.rem(x + k, wide)) * 2 + core
 
     barrier = pltpu.get_barrier_semaphore()
 
-    def greet(j, carry):
-        pl.semaphore_signal(
-            barrier, inc=1, device_id={"seq": lax.rem(seq + 2 * j, seq_count)}, device_id_type=MESH
-        )
-        return carry
-
-    lax.fori_loop(1, pairs, greet, 0)
+    def both_ways(act):
+        act(half)
+
+        def body(i, carry):
+            act(half - i)
+            act(half + i)
+            return carry
+
+        lax.fori_loop(1, half, body, 0)
+
+    both_ways(
+        lambda j: pl.semaphore_signal(barrier, inc=1, device_id={"seq": at_z(j)}, device_id_type=MESH)
+    )
+    for k in range(1, wide):
+        pl.semaphore_signal(barrier, inc=1, device_id={"seq": at_x(k)}, device_id_type=MESH)
     for off in (1, 2, 3):
         pl.semaphore_signal(barrier, inc=1, device_id={"head": peer(off)}, device_id_type=MESH)
     for side in (left, right, partner):
         pl.semaphore_signal(barrier, inc=1, device_id={"seq": side}, device_id_type=MESH)
 
     for h in range(HEADS_ALL):
-        gain_ref[h] = gain_all[:, h * PART : (h + 1) * PART]
+        gain_ref[h] = gain_all[h * PART : (h + 1) * PART][None, :]
     len_row[...] = jnp.zeros_like(len_row)
     len_row[0:1, 0 : len_ref.shape[1]] = len_ref[...].astype(f32)
     rows_i = lax.broadcasted_iota(jnp.int32, (F, F), 0)
     cols_i = lax.broadcasted_iota(jnp.int32, (F, F), 1)
-    pl.semaphore_wait(barrier, pairs + 5)
-
-    def slot_copy(j):
-        there = lax.rem(pair + j, pairs)
+    pl.semaphore_wait(barrier, deep + wide + 4)
+
+    def across(k):
         return remote(
-            loader.at[there], arr.at[pair], a_send.at[j], a_recv.at[j], {"seq": lax.rem(seq + 2 * j, seq_count)}
+            loader.at[:, lax.rem(x + k, wide)], xin.at[x], x_send.at[k], x_recv.at[k], {"seq": at_x(k)}
         )
 
-    def pass_on(j):
-        slot = lax.rem(pair + pairs - j, pairs)
-        return remote(arr.at[slot], par.at[slot], f_send.at[j], f_recv.at[j], {"seq": partner})
-
-    own_pass = remote(loader.at[pair], par.at[pair], f_send.at[0], f_recv.at[0], {"seq": partner})
-
-    def both_ways(act):
-        act(half)
-
-        def body(i, carry):
-            act(half - i)
-            act(half + i)
-            return carry
-
-        lax.fori_loop(1, half, body, 0)
-
-    both_ways(lambda j: slot_copy(j).start())
-    own_pass.start()
+    def held(k, layer):
+        came = lax.rem(x + wide - k, wide)
+        return xin.at[came, layer] if k else loader.at[layer, x]
+
+    def far(j, k):
+        came = lax.rem(x + wide - k, wide)
+        return remote(
+            held(k, lax.rem(z + j, deep)), arr.at[z, came],
+            z_send.at[k, j], z_recv.at[k, j], {"seq": at_z(j)},
+        )
+
+    def keep(k):
+        return pltpu.make_async_copy(held(k, z), arr.at[z, lax.rem(x + wide - k, wide)], l_sem.at[k])
+
+    def pass_on(j, k):
+        layer, came = lax.rem(z + deep - j, deep), lax.rem(x + wide - k, wide)
+        return remote(
+            arr.at[layer, came], par.at[layer, came], f_send.at[k, j], f_recv.at[k, j], {"seq": partner}
+        )
+
+    for k in steps[::-1]:
+        across(k).start()
+    both_ways(lambda j: far(j, 0).start())
+    keep(0).start()
+    for k in steps:
+        across(k).wait_recv()
+        both_ways(lambda j: far(j, k).start())
+        keep(k).start()
 
     lens = len_row[0:1, :]
     ends_col = jnp.sum(jnp.where(cols_i <= rows_i, lens, 0.0), axis=1, keepdims=True)
@@ -173,28 +196,45 @@
         target = jnp.where((slot_core == core) & (within < count), start + within, -1.0)
         hot[which] = (frame_rows == target).astype(f32).astype(bf16)
 
-    def land(j):
-        slot_copy(j).wait_recv()
-        pass_on(j).start()
-
-    both_ways(land)
-    own_tile.wait()
-    own_pass.wait_recv()
-    both_ways(lambda j: pass_on(j).wait_recv())
+    for k in [0] + steps:
+        keep(k).wait()
+        pass_on(0, k).start()
+
+        def land(j):
+            far(j, k).wait_recv()
+            pass_on(j, k).start()
+
+        both_ways(land)
+    for k in [0] + steps:
+        pass_on(0, k).wait_recv()
+        both_ways(lambda j: pass_on(j, k).wait_recv())
     frame_ref[...] = (
         mm(hot[0], arr[...].reshape(slots, PART)) + mm(hot[1], par[...].reshape(slots, PART))
     ).astype(bf16)
 
+    low, high = pl.ds(0, F // 2), pl.ds(F // 2, F // 2)
+    up, down_by = {"head": peer(1)}, {"head": peer(3)}
+
+    def gather_copy(i, src, slot, rows, where):
+        return remote(src, gath.at[slot, rows, :], ag_send.at[i], ag_recv.at[i], where)
+
     gathers = [
-        remote(frame_ref, gath.at[me], ag_send.at[off - 1], ag_recv.at[off - 1], {"head": peer(off)})
-        for off in (2, 1, 3)
+        gather_copy(0, frame_ref.at[low, :], me, low, up),
+        gather_copy(1, frame_ref.at[high, :], me, high, up),
+        gather_copy(2, frame_ref.at[high, :], me, high, down_by),
+        gather_copy(3, frame_ref.at[low, :], me, low, down_by),
+        gather_copy(4, gath.at[peer(3), low, :], peer(3), low, up),
+        gather_copy(5, gath.at[peer(1), high, :], peer(1), high, down_by),
     ]
-    for copy in gathers:
-        copy.start()
+    for i in (0, 2, 1, 3):
+        gathers[i].start()
     gath[me] = frame_ref[...]
-
-    for copy in gathers:
-        copy.wait_recv()
+    gathers[0].wait_recv()
+    gathers[4].start()
+    gathers[2].wait_recv()
+    gathers[5].start()
+    for i in (1, 3, 4, 5):
+        gathers[i].wait_recv()
 
     def norm_rows(r, carry):
         rows = pl.ds(pl.multiple_of(r * 32, 32), 32)
@@ -238,11 +278,10 @@
         return carry
 
     lax.fori_loop(0, GROUPS, own_scores, 0)
-    for copy in halos:
+    for copy in halos[:2]:
         copy.wait_recv()
 
-    def attend(g, carry):
-        parts = []
+    def weigh(g, carry):
         for sub in range(2):
             qm = qs[g] * mb[sub]
             score = [
@@ -255,14 +294,22 @@
             lifted = [jnp.exp(x - top) for x in score]
             total = jnp.sum(lifted[0] + lifted[1] + lifted[2], axis=1, keepdims=True)
             inv = 1.0 / total
-            acc = None
             for b in range(3):
                 w = lifted[b] * inv
                 wts[2 * g + sub, b] = w
-                low = w.astype(bf16)
-                wlow[2 * g + sub, b] = low
-                term = mm(low, kv[b, 1, g])
-                acc = term if acc is None else acc + term
+                wlow[2 * g + sub, b] = w.astype(bf16)
+        return carry
+
+    lax.fori_loop(0, GROUPS, weigh, 0)
+    for copy in halos[2:]:
+        copy.wait_recv()
+
+    def attend(g, carry):
+        parts = []
+        for sub in range(2):
+            acc = mm(wlow[2 * g + sub, 0], kv[0, 1, g])
+            for b in (1, 2):
+                acc = acc + mm(wlow[2 * g + sub, b], kv[b, 1, g])
             parts.append(acc * mf[sub])
         both = parts[0] + parts[1]
         att[g] = both
@@ -289,21 +336,22 @@
     for copy in res_edges:
         copy.start()
 
-    def taps(ext, g, r, mirrored):
+    def taps(ext, r, mirrored):
         base = seg_col[WIN + r : WIN + r + CHUNK, :]
-        acc = jnp.zeros((CHUNK, LANES), f32)
+        acc = [jnp.zeros((CHUNK, LANES), f32) for _ in range(GROUPS)]
         for t in range(KS):
             shift = (HALF_K - t) if mirrored else (t - HALF_K)
             same = seg_col[WIN + r + shift : WIN + r + shift + CHUNK, :] == base
-            term = ext[g, PAD + r + shift : PAD + r + shift + CHUNK, :] * cw_ref[t : t + 1, pl.ds(pl.multiple_of(g * LANES, LANES), LANES)]
-            acc = acc + jnp.where(same, term, 0.0)
+            for g in range(GROUPS):
+                term = ext[g, PAD + r + shift : PAD + r + shift + CHUNK, :]
+                term = term * cw_ref[t : t + 1, g * LANES : (g + 1) * LANES]
+                acc[g] = acc[g] + jnp.where(same, term, 0.0)
         return acc
 
     def forward_conv(starts):
-        def body(g, carry):
-            columns = pl.ds(pl.multiple_of(g * LANES, LANES), LANES)
-            for r in starts:
-                conv = taps(res_ext, g, r, False)
+        for r in starts:
+            for g, conv in enumerate(taps(res_ext, r, False)):
+                columns = slice(g * LANES, (g + 1) * LANES)
                 gate = lax.logistic(conv)
                 out_ref[r : r + CHUNK, columns] = (
                     res_ext[g, PAD + r : PAD + r + CHUNK, :] + conv * gate
@@ -312,20 +360,13 @@
                 gc = (up * gate * (1.0 + conv * (1.0 - gate))).astype(bf16)
                 gc_low[g, r : r + CHUNK, :] = gc
                 gc_ext[g, PAD + r : PAD + r + CHUNK, :] = gc.astype(f32)
-            return carry
-
-        lax.fori_loop(0, GROUPS, body, 0)
 
     def backward_conv(starts):
-        def body(g, carry):
-            columns = pl.ds(pl.multiple_of(g * LANES, LANES), LANES)
-            for r in starts:
-                moved = taps(gc_ext, g, r, True)
+        for r in starts:
+            for g, moved in enumerate(taps(gc_ext, r, True)):
+                columns = slice(g * LANES, (g + 1) * LANES)
                 up = cot_ref[r : r + CHUNK, columns].astype(f32)
                 gres[g, r : r + CHUNK, :] = (up + moved).astype(bf16)
-            return carry
-
-        lax.fori_loop(0, GROUPS, body, 0)
 
     inner = (CHUNK, 2 * CHUNK)
     outer = (0, 3 * CHUNK)
@@ -442,14 +483,46 @@
 
     lax.fori_loop(0, F // 32, finish, 0)
 
-    both_ways(lambda j: slot_copy(j).wait_send())
-    both_ways(lambda j: pass_on(j).wait_send())
-    own_pass.wait_send()
+    for k in [0] + steps:
+        if k:
+            across(k).wait_send()
+
+        def drain(j):
+            far(j, k).wait_send()
+            pass_on(j, k).wait_send()
+
+        both_ways(drain)
+        pass_on(0, k).wait_send()
     for copy in gathers + halos + res_edges + gc_edges + exchanges:
         copy.wait_send()
     for g in range(GROUPS):
         for copy in kv_grad_copies(g):
             copy.wait_send()
+
+
+def copy_kernel(a_ref, b_ref, c_ref, d_ref, held, came, gone):
+    ins = [pltpu.make_async_copy(r, held.at[i], came.at[i]) for i, r in enumerate((a_ref, b_ref))]
+    outs = [pltpu.make_async_copy(held.at[i], r, gone.at[i]) for i, r in enumerate((c_ref, d_ref))]
+    for copy in ins:
+        copy.start()
+    for i in range(2):
+        ins[i].wait()
+        outs[i].start()
+    for copy in outs:
+        copy.wait()
+
+
+def hand_out(results):
+    hbm = pl.BlockSpec(memory_space=pl.ANY)
+    shape = jax.ShapeDtypeStruct((F, PART), jnp.bfloat16)
+    dma = pltpu.SemaphoreType.DMA
+    return pl.pallas_call(
+        copy_kernel,
+        out_shape=(shape, shape),
+        in_specs=[hbm, hbm],
+        out_specs=(hbm, hbm),
+        scratch_shapes=[pltpu.VMEM((2, F, PART), jnp.bfloat16), dma((2,)), dma((2,))],
+    )(*results)
 
 
 def block_call(loader_rows, plan, lengths, gain, wq, wk, wv, conv_weight, cotangent):
@@ -459,7 +532,9 @@
     pairs = seq_count // 2
     tile = loader_rows.shape[0] // pairs
     slots = pairs * tile
-    loader = loader_rows.reshape(pairs, tile, PART)
+    wide = 4 if pairs > 8 else 2
+    deep = pairs // wide
+    loader = loader_rows.reshape(deep, wide, tile, PART)
     vmem = pl.BlockSpec(memory_space=pltpu.VMEM)
     hbm = pl.BlockSpec(memory_space=pl.ANY)
     v = pltpu.VMEM
@@ -471,8 +546,9 @@
         in_specs=[vmem] * 5 + [hbm] * 4,
         out_specs=(vmem, vmem),
         scratch_shapes=[
-            v((pairs, tile, PART), bf16),
-            v((pairs, tile, PART), bf16),
+            v((wide, deep, tile, PART), bf16),
+            v((deep, wide, tile, PART), bf16),
+            v((deep, wide, tile, PART), bf16),
             v((2, F, slots), bf16),
             v((8, F), f32),
             v((8, span), f32),
@@ -510,14 +586,16 @@
             v((3, F, PART), bf16),
             v((8, F), f32),
             v((3, 8, F), f32),
-            dma((pairs,)),
-            dma((pairs,)),
-            dma((pairs,)),
-            dma((pairs,)),
-            dma((1,)),
+            dma((wide, deep)),
+            dma((wide, deep)),
+            dma((wide,)),
+            dma((wide,)),
+            dma((wide,)),
+            dma((wide, deep)),
+            dma((wide, deep)),
             dma((3,)),
-            dma((3,)),
-            dma((3,)),
+            dma((6,)),
+            dma((6,)),
             dma((2, 2)),
             dma((2, 2)),
             dma((2,)),
@@ -534,11 +612,11 @@
         compiler_params=pltpu.CompilerParams(
             collective_id=0, has_side_effects=True, vmem_limit_bytes=56 * 1024 * 1024
         ),
-    )(plan, lengths[None, :], gain[None, :], conv_weight, cotangent, loader, wq, wk, wv)
+    )(plan, lengths[None, :], gain, conv_weight, cotangent, loader, wq, wk, wv)
 
 
 def on_device(loader_rows, plan, lengths, gain, wq, wk, wv, conv_weight, cotangent):
-    return block_call(loader_rows, plan, lengths, gain, wq, wk, wv, conv_weight, cotangent)
+    return hand_out(block_call(loader_rows, plan, lengths, gain, wq, wk, wv, conv_weight, cotangent))
 
 
 def solution(mesh):

time: 104 us -> 95.4 us (0.917)
  the two profiles are of different devices: /device:TPU:1 before, /device:TPU:8 now
where the time goes in v5:
time: 95.4 us; the launch traced here: 95.3 us
  Pallas kernels  94.6 us (99%)
    pallas_call x1, Pallas kernels, block_call(): pl.pallas_call(block_kernel, out_shape=(shape, shape), in_specs=[vmem] *...  92.9 us

profile of v5, /device:TPU:8, one launch (start us, length us, event | category | flops | bytes accessed | tf_op | source)
XLA Modules:
  0.0 95.3 jit_solution(4583640563128956055)
XLA Ops:
  0.6 92.9 %shard_map.104 = (bf16[256,384]{1,0:T(8,128)(2,1)}, bf16[256,384]{1,0:T(8,128)(2,1)}) custom-call(s32[128,128]{1,0:T(8,128)} %plan_ref.1, s32[1,170]{1,0:T(1,128)} %bitcast.3, f32[1536]{0:T(1024)} %gain_all.1, f32[31,384]{1,0:T(8,128)} %cw_ref.1, bf16[256,384]{1,0:T(8,128)(2,1)} %cot_ref.1, bf16[16,4,8,384]{3,2,1,0:T(8,128)(2,1)} %bitcast.2, ...), custom_call_target="tpu_custom_call" | custom-call | tf_op jit(solution)/shard_map/pallas_call | solution.py:543
  93.5 1.7 %shard_map.105 = (bf16[256,384]{1,0:T(8,128)(2,1)}, bf16[256,384]{1,0:T(8,128)(2,1)}) custom-call(bf16[256,384]{1,0:T(8,128)(2,1)} %get-tuple-element.4.a_ref, bf16[256,384]{1,0:T(8,128)(2,1)} %get-tuple-element.5.b_ref), custom_call_target="tpu_custom_call" | custom-call | tf_op jit(solution)/shard_map/pallas_call | solution.py:519

commit v6 on v5

--- a/solution.py
+++ b/solution.py
@@ -32,16 +32,12 @@
     return lax.dot_general(a, b, (((1,), (1,)), ((), ())), preferred_element_type=jnp.float32)
 
 
-def mm_tn(a, b):
-    return lax.dot_general(a, b, (((0,), (0,)), ((), ())), preferred_element_type=jnp.float32)
-
-
 def block_kernel(
     plan_ref, len_ref, gain_all, cw_ref, cot_ref, loader, wq_hbm, wk_hbm, wv_hbm,
     out_ref, grad_ref,
     xin, arr, par, hot, len_row, seg_row, seg_col, gain_ref, frame_ref, gath, unit, normed, inv_ref, wq, wk, wv, kv, qs, bias, wts, wlow, att,
     res_low, res_ext, res_halo, gc_low, gc_ext, gc_halo, gres,
-    dq_ref, dsend, drecv, down, dkb, dvb, pacc, psend, precv, ssend, srecv,
+    dq_ref, dq_part, dsend, drecv, down, dkb, dvb, pacc, psend, precv, ssend, srecv,
     z_send, z_recv, x_send, x_recv, l_sem, f_send, f_recv, w_sem, ag_send, ag_recv, kv_send, kv_recv, rh_send, rh_recv, gh_send, gh_recv,
     d_send, d_recv, p_send, p_recv, s_send, s_recv,
 ):
@@ -205,12 +201,11 @@
             pass_on(j, k).start()
 
         both_ways(land)
+    picked = mm(hot[0], arr[...].reshape(slots, PART))
     for k in [0] + steps:
         pass_on(0, k).wait_recv()
         both_ways(lambda j: pass_on(j, k).wait_recv())
-    frame_ref[...] = (
-        mm(hot[0], arr[...].reshape(slots, PART)) + mm(hot[1], par[...].reshape(slots, PART))
-    ).astype(bf16)
+    frame_ref[...] = (picked + mm(hot[1], par[...].reshape(slots, PART))).astype(bf16)
 
     low, high = pl.ds(0, F // 2), pl.ds(F // 2, F // 2)
     up, down_by = {"head": peer(1)}, {"head": peer(3)}
@@ -390,37 +385,51 @@
             remote(dsend.at[1, g], drecv.at[0, g], d_send.at[1, g], d_recv.at[0, g], {"seq": right}),
         ]
 
-    def attend_back(g, carry):
-        gq = []
-        dk = [None, None, None]
-        dv = [None, None, None]
-        for sub in range(2):
-            gm = gres[g] * mb[sub]
-            qm = qs[g] * mb[sub]
-            delta = jnp.sum(gm.astype(f32) * att[g], axis=1, keepdims=True)
-            acc = None
-            for b in range(3):
-                gw = mm_nt(gm, kv[b, 1, g])
-                ds = (wts[2 * g + sub, b] * (gw - delta) * scale).astype(bf16)
-                term = mm(ds, kv[b, 0, g])
-                acc = term if acc is None else acc + term
-                dkt = mm_tn(ds, qm)
-                dvt = mm_tn(wlow[2 * g + sub, b], gm)
-                dk[b] = dkt if dk[b] is None else dk[b] + dkt
-                dv[b] = dvt if dv[b] is None else dv[b] + dvt
-            gq.append(acc * mf[sub])
-        columns = pl.ds(pl.multiple_of(g * LANES, LANES), LANES)
-        dq_ref[:, columns] = (gq[0] + gq[1]).astype(bf16)
-        for slot, b in ((0, 0), (1, 2)):
-            dsend[slot, g, 0] = dk[b].astype(bf16)
-            dsend[slot, g, 1] = dv[b].astype(bf16)
-        down[g, 0] = dk[1]
-        down[g, 1] = dv[1]
-        for copy in kv_grad_copies(g):
-            copy.start()
-        return carry
-
-    lax.fori_loop(0, GROUPS, attend_back, 0)
+    rows_lane = lax.broadcasted_iota(jnp.int32, (LANES, 1), 0)
+    mt = [(rows_lane < HEAD_DIM).astype(f32), (rows_lane >= HEAD_DIM).astype(f32)]
+
+    def attend_back(blocks):
+        def body(g, carry):
+            q_turned = jnp.transpose(qs[g].astype(f32))
+            g_turned = jnp.transpose(gres[g].astype(f32))
+            gq = []
+            dk = {b: None for b in blocks}
+            dv = {b: None for b in blocks}
+            for sub in range(2):
+                gm = gres[g] * mb[sub]
+                qt = (q_turned * mt[sub]).astype(bf16)
+                gt = (g_turned * mt[sub]).astype(bf16)
+                delta = jnp.sum(gm.astype(f32) * att[g], axis=1, keepdims=True)
+                acc = None
+                for b in blocks:
+                    gw = mm_nt(gm, kv[b, 1, g])
+                    ds = (wts[2 * g + sub, b] * (gw - delta) * scale).astype(bf16)
+                    term = mm(ds, kv[b, 0, g])
+                    acc = term if acc is None else acc + term
+                    dkt = mm(qt, ds)
+                    dvt = mm(gt, wlow[2 * g + sub, b])
+                    dk[b] = dkt if dk[b] is None else dk[b] + dkt
+                    dv[b] = dvt if dv[b] is None else dv[b] + dvt
+                gq.append(acc * mf[sub])
+            gq = gq[0] + gq[1]
+            columns = pl.ds(pl.multiple_of(g * LANES, LANES), LANES)
+            if blocks == (1,):
+                dq_ref[:, columns] = (gq + dq_part[g]).astype(bf16)
+                down[g, 0] = dk[1]
+                down[g, 1] = dv[1]
+            else:
+                dq_part[g] = gq
+                for slot, b in ((0, 0), (1, 2)):
+                    dsend[slot, g, 0] = dk[b].astype(bf16)
+                    dsend[slot, g, 1] = dv[b].astype(bf16)
+                for copy in kv_grad_copies(g):
+                    copy.start()
+            return carry
+
+        lax.fori_loop(0, GROUPS, body, 0)
+
+    attend_back((0, 2))
+    attend_back((1,))
 
     def weight_rows(ref, off):
         return ref[pl.ds(pl.multiple_of(peer(off) * PART, PART), PART), :]
@@ -432,9 +441,8 @@
         for copy in kv_grad_copies(g):
             copy.wait_recv()
         for which, dst in ((0, dkb), (1, dvb)):
-            dst[:, g * LANES : (g + 1) * LANES] = (
-                down[g, which] + drecv[0, g, which].astype(f32) + drecv[1, g, which].astype(f32)
-            ).astype(bf16)
+            summed = down[g, which] + drecv[0, g, which].astype(f32) + drecv[1, g, which].astype(f32)
+            dst[:, g * LANES : (g + 1) * LANES] = jnp.transpose(summed).astype(bf16)
 
     row_sum = jnp.zeros((F, 1), f32)
     row_dot = jnp.zeros((F, 1), f32)
@@ -576,9 +584,10 @@
             v((2, GROUPS, PAD, LANES), bf16),
             v((GROUPS, F, LANES), bf16),
             v((F, PART), bf16),
-            v((2, GROUPS, 2, F, LANES), bf16),
-            v((2, GROUPS, 2, F, LANES), bf16),
-            v((GROUPS, 2, F, LANES), f32),
+            v((GROUPS, F, LANES), f32),
+            v((2, GROUPS, 2, LANES, F), bf16),
+            v((2, GROUPS, 2, LANES, F), bf16),
+            v((GROUPS, 2, LANES, F), f32),
             v((F, PART), bf16),
             v((F, PART), bf16),
             v((HEADS_ALL, F, PART), f32),

time: 95.4 us -> 94.4 us (0.990)
  Pallas kernels: 94.6 us -> 93.6 us
    pallas_call x1, Pallas kernels: 92.9 us -> 91.9 us  [block_call(): pl.pallas_call(block_kernel, out_shape=(shape, shape), in_specs=[vmem] *...]
where the time goes in v6:
time: 94.4 us; the launch traced here: 94.3 us
  Pallas kernels  93.6 us (99%)
    pallas_call x1, Pallas kernels, block_call(): pl.pallas_call(block_kernel, out_shape=(shape, shape), in_specs=[vmem] *...  91.9 us

profile of v6, /device:TPU:8, one launch (start us, length us, event | category | flops | bytes accessed | tf_op | source)
XLA Modules:
  0.0 94.3 jit_solution(12128785898581354254)
XLA Ops:
  0.6 91.9 %shard_map.104 = (bf16[256,384]{1,0:T(8,128)(2,1)}, bf16[256,384]{1,0:T(8,128)(2,1)}) custom-call(s32[128,128]{1,0:T(8,128)} %plan_ref.1, s32[1,170]{1,0:T(1,128)} %bitcast.3, f32[1536]{0:T(1024)} %gain_all.1, f32[31,384]{1,0:T(8,128)} %cw_ref.1, bf16[256,384]{1,0:T(8,128)(2,1)} %cot_ref.1, bf16[16,4,8,384]{3,2,1,0:T(8,128)(2,1)} %bitcast.2, ...), custom_call_target="tpu_custom_call" | custom-call | tf_op jit(solution)/shard_map/pallas_call | solution.py:551
  92.5 1.7 %shard_map.105 = (bf16[256,384]{1,0:T(8,128)(2,1)}, bf16[256,384]{1,0:T(8,128)(2,1)}) custom-call(bf16[256,384]{1,0:T(8,128)(2,1)} %get-tuple-element.4.a_ref, bf16[256,384]{1,0:T(8,128)(2,1)} %get-tuple-element.5.b_ref), custom_call_target="tpu_custom_call" | custom-call | tf_op jit(solution)/shard_map/pallas_call | solution.py:527

commit v7 on v6

--- a/solution.py
+++ b/solution.py
@@ -450,8 +450,7 @@
     for off in (2, 1, 3, 0):
         part = pacc[off] + mm_nt(dkb[...], weight_rows(wk, off)) + mm_nt(dvb[...], weight_rows(wv, off))
         part = part * gain_ref[peer(off)]
-        row_sum = row_sum + jnp.sum(part, axis=1, keepdims=True)
-        row_dot = row_dot + jnp.sum(part * unit[peer(off)], axis=1, keepdims=True)
+        pacc[off] = part
         if off:
             psend[off - 1] = part.astype(bf16)
             copy = remote(
@@ -459,8 +458,10 @@
             )
             copy.start()
             exchanges.append(copy)
-        else:
-            pacc[0] = part
+    for off in range(HEADS_ALL):
+        part = pacc[off]
+        row_sum = row_sum + jnp.sum(part, axis=1, keepdims=True)
+        row_dot = row_dot + jnp.sum(part * unit[peer(off)], axis=1, keepdims=True)
 
     lanes = lax.broadcasted_iota(jnp.int32, (F, LANES), 1)
     packed = jnp.where(lanes == 0, row_sum, jnp.where(lanes == 1, row_dot, 0.0))

time: 94.4 us -> 94.4 us (level)
  no operation moved by 1% of the time
where the time goes in v7:
time: 94.4 us; the launch traced here: 94.2 us
  Pallas kernels  93.6 us (99%)
    pallas_call x1, Pallas kernels, block_call(): pl.pallas_call(block_kernel, out_shape=(shape, shape), in_specs=[vmem] *...  91.9 us

profile of v7, /device:TPU:8, one launch (start us, length us, event | category | flops | bytes accessed | tf_op | source)
XLA Modules:
  0.0 94.2 jit_solution(2483705127359112666)
XLA Ops:
  0.6 91.9 %shard_map.104 = (bf16[256,384]{1,0:T(8,128)(2,1)}, bf16[256,384]{1,0:T(8,128)(2,1)}) custom-call(s32[128,128]{1,0:T(8,128)} %plan_ref.1, s32[1,170]{1,0:T(1,128)} %bitcast.3, f32[1536]{0:T(1024)} %gain_all.1, f32[31,384]{1,0:T(8,128)} %cw_ref.1, bf16[256,384]{1,0:T(8,128)(2,1)} %cot_ref.1, bf16[16,4,8,384]{3,2,1,0:T(8,128)(2,1)} %bitcast.2, ...), custom_call_target="tpu_custom_call" | custom-call | tf_op jit(solution)/shard_map/pallas_call | solution.py:552
  92.5 1.7 %shard_map.105 = (bf16[256,384]{1,0:T(8,128)(2,1)}, bf16[256,384]{1,0:T(8,128)(2,1)}) custom-call(bf16[256,384]{1,0:T(8,128)(2,1)} %get-tuple-element.4.a_ref, bf16[256,384]{1,0:T(8,128)(2,1)} %get-tuple-element.5.b_ref), custom_call_target="tpu_custom_call" | custom-call | tf_op jit(solution)/shard_map/pallas_call | solution.py:528
